TPU v7x, 256 devices: a whole 4x4x8 slice. The times are simulated.
256 devices in a mesh: chan: 8 (over y, core), dm: 8 (over z), bin: 4 (over x).
Axes of the slice: x: 4, y: 4, z: 8, core: 2. Of those that a mesh axis runs over, the one named last changes fastest.
Arguments:
- spectra: bfloat16 [2, 4, 8192, 4096], P(None, None, ('chan', 'dm'), 'bin'), may hold values from -6 to 6
- delays: int32 [8192, 64], P(('chan', 'dm')), may hold values from 0 to 8191
- templates: bfloat16 [2, 64, 64], replicated, may hold values from -0.5 to 0.5
Outputs:
- power: bfloat16 [64, 64, 4, 4096], P(('chan', 'dm'), None, None, 'bin')
All inputs are finite; a program needn't handle non-finite values.
Results may differ from a plain program's by a relative error of at most 0.01.
Values may be sent and summed in bfloat16 or wider, within the bound.
No kernel may reach another device: no remote copies, remote signals or barrier semaphores. Data moves between devices by JAX's collectives and lax.ppermute only.
A program may use at most 64 MiB of HBM per device.

v0:
```python
import math

import jax
import jax.numpy as jnp
from jax import lax
from jax.sharding import PartitionSpec as P

D = 64
TEMPLATES = 64
TAPS = 64


def extended_2(cells, sides, width):
    for axis, dim in sides:
        count = lax.axis_size(axis)
        ends = count - 1
        head = lax.slice_in_dim(cells, 0, width, axis=dim)
        tail = lax.slice_in_dim(cells, cells.shape[dim] - width, cells.shape[dim], axis=dim)
        cells = jnp.concatenate(
            [
                lax.ppermute(tail, axis, [(i, (i + 1) % count) for i in range(ends)]),
                cells,
                lax.ppermute(head, axis, [((i + 1) % count, i) for i in range(ends)]),
            ],
            axis=dim,
        )
    return cells


def rotation(delay_rows, bin_index, period, half_period):
    product = delay_rows[:, :, None] * bin_index[None, None, :] % period
    theta = product.astype(jnp.float32) * (jnp.pi / half_period)
    return (jnp.cos(theta), -jnp.sin(theta))


def shards(spectra, delays, templates):
    bin_width = spectra.shape[3]
    total_chan = spectra.shape[2] * lax.axis_size(("chan", "dm"))
    half_period = bin_width * lax.axis_size("bin")
    period = 2 * half_period
    bin_first = lax.axis_index("bin") * bin_width
    norm_scale = 1.0 / math.sqrt(total_chan)
    block_width = min(128, bin_width)
    block_total = bin_width // block_width
    weight_real = jnp.stack([templates[0], -templates[1]], axis=1)
    weight_imag = jnp.stack([templates[1], templates[0]], axis=1)
    tap_weights = jnp.concatenate([weight_real, weight_imag], axis=0)
    beam_total = spectra.shape[1]
    empty = jnp.zeros(
        (
            D // lax.axis_size(("chan", "dm")) * lax.axis_size(("chan", "dm")),
            2,
            beam_total,
            bin_width,
        ),
        jnp.float32,
    )

    def one_block(position, buffer):
        offset = position * block_width
        first_bin = bin_first + offset
        bins = first_bin + jnp.arange(block_width, dtype=jnp.int32)
        phase_re, phase_im = rotation(delays, bins, period, half_period)
        phase_re = phase_re.astype(jnp.bfloat16)
        phase_im = phase_im.astype(jnp.bfloat16)
        piece = lax.dynamic_slice_in_dim(spectra, offset, block_width, 3)
        real_sum = jnp.einsum(
            "bck,cdk->dbk", piece[0], phase_re, preferred_element_type=jnp.float32
        ) - jnp.einsum("bck,cdk->dbk", piece[1], phase_im, preferred_element_type=jnp.float32)
        imag_sum = jnp.einsum(
            "bck,cdk->dbk", piece[0], phase_im, preferred_element_type=jnp.float32
        ) + jnp.einsum("bck,cdk->dbk", piece[1], phase_re, preferred_element_type=jnp.float32)
        block_term = jnp.stack([real_sum, imag_sum], axis=1) * norm_scale
        return lax.dynamic_update_slice_in_dim(buffer, block_term, offset, 3)

    summed = lax.psum_scatter(
        lax.fori_loop(0, block_total, one_block, empty),
        ("chan", "dm"),
        scatter_dimension=0,
        tiled=True,
    )
    extended = extended_2(summed.astype(jnp.bfloat16), (("bin", 3),), TAPS // 2)
    windows = jnp.stack(
        [extended[:, :, :, shift_by : shift_by + bin_width] for shift_by in range(TAPS)], axis=2
    )
    response = jnp.einsum(
        "oct,dctbk->dobk", tap_weights, windows, preferred_element_type=jnp.float32
    )
    real_part = response[:, :TEMPLATES]
    imag_part = response[:, TEMPLATES:]
    return (real_part * real_part + imag_part * imag_part).astype(jnp.bfloat16)


def solution(mesh):
    placed = (P(None, None, ("chan", "dm"), "bin"), P(("chan", "dm"), None), P())
    return jax.shard_map(
        shards,
        mesh=mesh,
        in_specs=placed,
        out_specs=P(("chan", "dm"), None, None, "bin"),
        check_vma=False,
    )
```

profile of v0, /device:TPU:6, one launch (start us, length us, event | category | flops | bytes accessed | tf_op | source)
XLA Modules:
  0.0 844.1 jit_solution(8408675928483416751)
XLA Ops:
  0.8 554.4 %while.15 = (s32[]{:T(128)}, f32[64,2,4,1024]{3,2,1,0:T(4,128)S(1)}, s32[128,64]{0,1:T(8,128)S(1)}, s32[]{:T(128)}, bf16[2,4,128,1024]{3,2,1,0:T(8,128)(2,1)}, /...) while((s32[]{:T(128)}, f32[64,2,4,1024]{3,2,1,0:T(4,128)S(1)}, s32[128,64]{0,1:T(8,128)S(1)}, ...), condition=%wide.region_1.2_spmd, body=%wide.region_0.1_spmd.sunk | while | flops 98762888 | bytes 4065979 | solution.py:77
  1.9 16.7 %fusion.150 = f32[128,64,4]{1,2,0:T(4,128)S(1)} fusion(s32[128]{0:T(128)S(1)} %iota_add_fusion.2, s32[128,64]{0,1:T(8,128)S(1)} %get-tuple-element.440, bf16[1,4,128,128]{2,1,3,0:T(4,128)(2,1)S(1)} %copy.2825), kind=kOutput, calls=%fused_computation.11.clone.1 | convolution fusion | flops 24117248 | bytes 295424 | tf_op jit(solution)/shard_map/while/body/eval_jaxpr/bck,cdk->dbk/dot_general | solution.py:67
  18.8 17.0 %fusion.151 = f32[64,1,4,128]{0,2,3,1:T(4,128)S(1)} fusion(f32[128,64,4]{1,2,0:T(4,128)S(1)} %fusion.150, s32[128]{0:T(128)S(1)} %iota_add_fusion.2, s32[128,64]{0,1:T(8,128)S(1)} %get-tuple-element.440, bf16[1,4,128,128]{2,1,3,0:T(4,128)(2,1)S(1)} %copy.2824), kind=kOutput, calls=%fused_computation.15.clone.1 | convolution fusion | flops 25198592 | bytes 426496 | tf_op jit(solution)/shard_map/while/body/eval_jaxpr/bck,cdk->dbk/dot_general | solution.py:69
  35.8 16.7 %fusion.148 = f32[128,64,4]{1,2,0:T(4,128)S(1)} fusion(s32[128]{0:T(128)S(1)} %iota_add_fusion.2, s32[128,64]{0,1:T(8,128)S(1)} %get-tuple-element.440, bf16[1,4,128,128]{2,1,3,0:T(4,128)(2,1)S(1)} %copy.2824), kind=kOutput, calls=%fused_computation.10.clone.1 | convolution fusion | flops 24117248 | bytes 295424 | tf_op jit(solution)/shard_map/while/body/eval_jaxpr/bck,cdk->dbk/dot_general | solution.py:72
  52.5 17.0 %fusion.149 = f32[64,1,4,128]{0,2,3,1:T(4,128)S(1)} fusion(f32[128,64,4]{1,2,0:T(4,128)S(1)} %fusion.148, s32[128]{0:T(128)S(1)} %iota_add_fusion.2, s32[128,64]{0,1:T(8,128)S(1)} %get-tuple-element.440, bf16[1,4,128,128]{2,1,3,0:T(4,128)(2,1)S(1)} %copy.2825), kind=kOutput, calls=%fused_computation.17.clone.1 | convolution fusion | flops 25198592 | bytes 426496 | tf_op jit(solution)/shard_map/while/body/eval_jaxpr/bck,cdk->dbk/dot_general | solution.py:70
  71.2 16.7 %fusion.150 = f32[128,64,4]{1,2,0:T(4,128)S(1)} fusion(s32[128]{0:T(128)S(1)} %iota_add_fusion.2, s32[128,64]{0,1:T(8,128)S(1)} %get-tuple-element.440, bf16[1,4,128,128]{2,1,3,0:T(4,128)(2,1)S(1)} %copy.2825), kind=kOutput, calls=%fused_computation.11.clone.1 | convolution fusion | flops 24117248 | bytes 295424 | tf_op jit(solution)/shard_map/while/body/eval_jaxpr/bck,cdk->dbk/dot_general | solution.py:67
  88.1 17.0 %fusion.151 = f32[64,1,4,128]{0,2,3,1:T(4,128)S(1)} fusion(f32[128,64,4]{1,2,0:T(4,128)S(1)} %fusion.150, s32[128]{0:T(128)S(1)} %iota_add_fusion.2, s32[128,64]{0,1:T(8,128)S(1)} %get-tuple-element.440, bf16[1,4,128,128]{2,1,3,0:T(4,128)(2,1)S(1)} %copy.2824), kind=kOutput, calls=%fused_computation.15.clone.1 | convolution fusion | flops 25198592 | bytes 426496 | tf_op jit(solution)/shard_map/while/body/eval_jaxpr/bck,cdk->dbk/dot_general | solution.py:69
  105.1 16.7 %fusion.148 = f32[128,64,4]{1,2,0:T(4,128)S(1)} fusion(s32[128]{0:T(128)S(1)} %iota_add_fusion.2, s32[128,64]{0,1:T(8,128)S(1)} %get-tuple-element.440, bf16[1,4,128,128]{2,1,3,0:T(4,128)(2,1)S(1)} %copy.2824), kind=kOutput, calls=%fused_computation.10.clone.1 | convolution fusion | flops 24117248 | bytes 295424 | tf_op jit(solution)/shard_map/while/body/eval_jaxpr/bck,cdk->dbk/dot_general | solution.py:72
  121.8 17.0 %fusion.149 = f32[64,1,4,128]{0,2,3,1:T(4,128)S(1)} fusion(f32[128,64,4]{1,2,0:T(4,128)S(1)} %fusion.148, s32[128]{0:T(128)S(1)} %iota_add_fusion.2, s32[128,64]{0,1:T(8,128)S(1)} %get-tuple-element.440, bf16[1,4,128,128]{2,1,3,0:T(4,128)(2,1)S(1)} %copy.2825), kind=kOutput, calls=%fused_computation.17.clone.1 | convolution fusion | flops 25198592 | bytes 426496 | tf_op jit(solution)/shard_map/while/body/eval_jaxpr/bck,cdk->dbk/dot_general | solution.py:70
  140.5 16.7 %fusion.150 = f32[128,64,4]{1,2,0:T(4,128)S(1)} fusion(s32[128]{0:T(128)S(1)} %iota_add_fusion.2, s32[128,64]{0,1:T(8,128)S(1)} %get-tuple-element.440, bf16[1,4,128,128]{2,1,3,0:T(4,128)(2,1)S(1)} %copy.2825), kind=kOutput, calls=%fused_computation.11.clone.1 | convolution fusion | flops 24117248 | bytes 295424 | tf_op jit(solution)/shard_map/while/body/eval_jaxpr/bck,cdk->dbk/dot_general | solution.py:67
  157.4 17.0 %fusion.151 = f32[64,1,4,128]{0,2,3,1:T(4,128)S(1)} fusion(f32[128,64,4]{1,2,0:T(4,128)S(1)} %fusion.150, s32[128]{0:T(128)S(1)} %iota_add_fusion.2, s32[128,64]{0,1:T(8,128)S(1)} %get-tuple-element.440, bf16[1,4,128,128]{2,1,3,0:T(4,128)(2,1)S(1)} %copy.2824), kind=kOutput, calls=%fused_computation.15.clone.1 | convolution fusion | flops 25198592 | bytes 426496 | tf_op jit(solution)/shard_map/while/body/eval_jaxpr/bck,cdk->dbk/dot_general | solution.py:69
  174.4 16.7 %fusion.148 = f32[128,64,4]{1,2,0:T(4,128)S(1)} fusion(s32[128]{0:T(128)S(1)} %iota_add_fusion.2, s32[128,64]{0,1:T(8,128)S(1)} %get-tuple-element.440, bf16[1,4,128,128]{2,1,3,0:T(4,128)(2,1)S(1)} %copy.2824), kind=kOutput, calls=%fused_computation.10.clone.1 | convolution fusion | flops 24117248 | bytes 295424 | tf_op jit(solution)/shard_map/while/body/eval_jaxpr/bck,cdk->dbk/dot_general | solution.py:72
  191.1 17.0 %fusion.149 = f32[64,1,4,128]{0,2,3,1:T(4,128)S(1)} fusion(f32[128,64,4]{1,2,0:T(4,128)S(1)} %fusion.148, s32[128]{0:T(128)S(1)} %iota_add_fusion.2, s32[128,64]{0,1:T(8,128)S(1)} %get-tuple-element.440, bf16[1,4,128,128]{2,1,3,0:T(4,128)(2,1)S(1)} %copy.2825), kind=kOutput, calls=%fused_computation.17.clone.1 | convolution fusion | flops 25198592 | bytes 426496 | tf_op jit(solution)/shard_map/while/body/eval_jaxpr/bck,cdk->dbk/dot_general | solution.py:70
  209.8 16.7 %fusion.150 = f32[128,64,4]{1,2,0:T(4,128)S(1)} fusion(s32[128]{0:T(128)S(1)} %iota_add_fusion.2, s32[128,64]{0,1:T(8,128)S(1)} %get-tuple-element.440, bf16[1,4,128,128]{2,1,3,0:T(4,128)(2,1)S(1)} %copy.2825), kind=kOutput, calls=%fused_computation.11.clone.1 | convolution fusion | flops 24117248 | bytes 295424 | tf_op jit(solution)/shard_map/while/body/eval_jaxpr/bck,cdk->dbk/dot_general | solution.py:67
  226.7 17.0 %fusion.151 = f32[64,1,4,128]{0,2,3,1:T(4,128)S(1)} fusion(f32[128,64,4]{1,2,0:T(4,128)S(1)} %fusion.150, s32[128]{0:T(128)S(1)} %iota_add_fusion.2, s32[128,64]{0,1:T(8,128)S(1)} %get-tuple-element.440, bf16[1,4,128,128]{2,1,3,0:T(4,128)(2,1)S(1)} %copy.2824), kind=kOutput, calls=%fused_computation.15.clone.1 | convolution fusion | flops 25198592 | bytes 426496 | tf_op jit(solution)/shard_map/while/body/eval_jaxpr/bck,cdk->dbk/dot_general | solution.py:69
  260.4 17.0 %fusion.149 = f32[64,1,4,128]{0,2,3,1:T(4,128)S(1)} fusion(f32[128,64,4]{1,2,0:T(4,128)S(1)} %fusion.148, s32[128]{0:T(128)S(1)} %iota_add_fusion.2, s32[128,64]{0,1:T(8,128)S(1)} %get-tuple-element.440, bf16[1,4,128,128]{2,1,3,0:T(4,128)(2,1)S(1)} %copy.2825), kind=kOutput, calls=%fused_computation.17.clone.1 | convolution fusion | flops 25198592 | bytes 426496 | tf_op jit(solution)/shard_map/while/body/eval_jaxpr/bck,cdk->dbk/dot_general | solution.py:70
  279.2 16.7 %fusion.150 = f32[128,64,4]{1,2,0:T(4,128)S(1)} fusion(s32[128]{0:T(128)S(1)} %iota_add_fusion.2, s32[128,64]{0,1:T(8,128)S(1)} %get-tuple-element.440, bf16[1,4,128,128]{2,1,3,0:T(4,128)(2,1)S(1)} %copy.2825), kind=kOutput, calls=%fused_computation.11.clone.1 | convolution fusion | flops 24117248 | bytes 295424 | tf_op jit(solution)/shard_map/while/body/eval_jaxpr/bck,cdk->dbk/dot_general | solution.py:67
  296.0 17.0 %fusion.151 = f32[64,1,4,128]{0,2,3,1:T(4,128)S(1)} fusion(f32[128,64,4]{1,2,0:T(4,128)S(1)} %fusion.150, s32[128]{0:T(128)S(1)} %iota_add_fusion.2, s32[128,64]{0,1:T(8,128)S(1)} %get-tuple-element.440, bf16[1,4,128,128]{2,1,3,0:T(4,128)(2,1)S(1)} %copy.2824), kind=kOutput, calls=%fused_computation.15.clone.1 | convolution fusion | flops 25198592 | bytes 426496 | tf_op jit(solution)/shard_map/while/body/eval_jaxpr/bck,cdk->dbk/dot_general | solution.py:69
  313.0 16.7 %fusion.148 = f32[128,64,4]{1,2,0:T(4,128)S(1)} fusion(s32[128]{0:T(128)S(1)} %iota_add_fusion.2, s32[128,64]{0,1:T(8,128)S(1)} %get-tuple-element.440, bf16[1,4,128,128]{2,1,3,0:T(4,128)(2,1)S(1)} %copy.2824), kind=kOutput, calls=%fused_computation.10.clone.1 | convolution fusion | flops 24117248 | bytes 295424 | tf_op jit(solution)/shard_map/while/body/eval_jaxpr/bck,cdk->dbk/dot_general | solution.py:72
  329.7 17.0 %fusion.149 = f32[64,1,4,128]{0,2,3,1:T(4,128)S(1)} fusion(f32[128,64,4]{1,2,0:T(4,128)S(1)} %fusion.148, s32[128]{0:T(128)S(1)} %iota_add_fusion.2, s32[128,64]{0,1:T(8,128)S(1)} %get-tuple-element.440, bf16[1,4,128,128]{2,1,3,0:T(4,128)(2,1)S(1)} %copy.2825), kind=kOutput, calls=%fused_computation.17.clone.1 | convolution fusion | flops 25198592 | bytes 426496 | tf_op jit(solution)/shard_map/while/body/eval_jaxpr/bck,cdk->dbk/dot_general | solution.py:70
  348.5 16.7 %fusion.150 = f32[128,64,4]{1,2,0:T(4,128)S(1)} fusion(s32[128]{0:T(128)S(1)} %iota_add_fusion.2, s32[128,64]{0,1:T(8,128)S(1)} %get-tuple-element.440, bf16[1,4,128,128]{2,1,3,0:T(4,128)(2,1)S(1)} %copy.2825), kind=kOutput, calls=%fused_computation.11.clone.1 | convolution fusion | flops 24117248 | bytes 295424 | tf_op jit(solution)/shard_map/while/body/eval_jaxpr/bck,cdk->dbk/dot_general | solution.py:67
  365.3 17.0 %fusion.151 = f32[64,1,4,128]{0,2,3,1:T(4,128)S(1)} fusion(f32[128,64,4]{1,2,0:T(4,128)S(1)} %fusion.150, s32[128]{0:T(128)S(1)} %iota_add_fusion.2, s32[128,64]{0,1:T(8,128)S(1)} %get-tuple-element.440, bf16[1,4,128,128]{2,1,3,0:T(4,128)(2,1)S(1)} %copy.2824), kind=kOutput, calls=%fused_computation.15.clone.1 | convolution fusion | flops 25198592 | bytes 426496 | tf_op jit(solution)/shard_map/while/body/eval_jaxpr/bck,cdk->dbk/dot_general | solution.py:69
  382.4 16.7 %fusion.148 = f32[128,64,4]{1,2,0:T(4,128)S(1)} fusion(s32[128]{0:T(128)S(1)} %iota_add_fusion.2, s32[128,64]{0,1:T(8,128)S(1)} %get-tuple-element.440, bf16[1,4,128,128]{2,1,3,0:T(4,128)(2,1)S(1)} %copy.2824), kind=kOutput, calls=%fused_computation.10.clone.1 | convolution fusion | flops 24117248 | bytes 295424 | tf_op jit(solution)/shard_map/while/body/eval_jaxpr/bck,cdk->dbk/dot_general | solution.py:72
  399.0 17.0 %fusion.149 = f32[64,1,4,128]{0,2,3,1:T(4,128)S(1)} fusion(f32[128,64,4]{1,2,0:T(4,128)S(1)} %fusion.148, s32[128]{0:T(128)S(1)} %iota_add_fusion.2, s32[128,64]{0,1:T(8,128)S(1)} %get-tuple-element.440, bf16[1,4,128,128]{2,1,3,0:T(4,128)(2,1)S(1)} %copy.2825), kind=kOutput, calls=%fused_computation.17.clone.1 | convolution fusion | flops 25198592 | bytes 426496 | tf_op jit(solution)/shard_map/while/body/eval_jaxpr/bck,cdk->dbk/dot_general | solution.py:70
  417.8 16.7 %fusion.150 = f32[128,64,4]{1,2,0:T(4,128)S(1)} fusion(s32[128]{0:T(128)S(1)} %iota_add_fusion.2, s32[128,64]{0,1:T(8,128)S(1)} %get-tuple-element.440, bf16[1,4,128,128]{2,1,3,0:T(4,128)(2,1)S(1)} %copy.2825), kind=kOutput, calls=%fused_computation.11.clone.1 | convolution fusion | flops 24117248 | bytes 295424 | tf_op jit(solution)/shard_map/while/body/eval_jaxpr/bck,cdk->dbk/dot_general | solution.py:67
  434.6 17.0 %fusion.151 = f32[64,1,4,128]{0,2,3,1:T(4,128)S(1)} fusion(f32[128,64,4]{1,2,0:T(4,128)S(1)} %fusion.150, s32[128]{0:T(128)S(1)} %iota_add_fusion.2, s32[128,64]{0,1:T(8,128)S(1)} %get-tuple-element.440, bf16[1,4,128,128]{2,1,3,0:T(4,128)(2,1)S(1)} %copy.2824), kind=kOutput, calls=%fused_computation.15.clone.1 | convolution fusion | flops 25198592 | bytes 426496 | tf_op jit(solution)/shard_map/while/body/eval_jaxpr/bck,cdk->dbk/dot_general | solution.py:69
  468.4 17.0 %fusion.149 = f32[64,1,4,128]{0,2,3,1:T(4,128)S(1)} fusion(f32[128,64,4]{1,2,0:T(4,128)S(1)} %fusion.148, s32[128]{0:T(128)S(1)} %iota_add_fusion.2, s32[128,64]{0,1:T(8,128)S(1)} %get-tuple-element.440, bf16[1,4,128,128]{2,1,3,0:T(4,128)(2,1)S(1)} %copy.2825), kind=kOutput, calls=%fused_computation.17.clone.1 | convolution fusion | flops 25198592 | bytes 426496 | tf_op jit(solution)/shard_map/while/body/eval_jaxpr/bck,cdk->dbk/dot_general | solution.py:70
  487.1 16.7 %fusion.150 = f32[128,64,4]{1,2,0:T(4,128)S(1)} fusion(s32[128]{0:T(128)S(1)} %iota_add_fusion.2, s32[128,64]{0,1:T(8,128)S(1)} %get-tuple-element.440, bf16[1,4,128,128]{2,1,3,0:T(4,128)(2,1)S(1)} %copy.2825), kind=kOutput, calls=%fused_computation.11.clone.1 | convolution fusion | flops 24117248 | bytes 295424 | tf_op jit(solution)/shard_map/while/body/eval_jaxpr/bck,cdk->dbk/dot_general | solution.py:67
  503.9 17.0 %fusion.151 = f32[64,1,4,128]{0,2,3,1:T(4,128)S(1)} fusion(f32[128,64,4]{1,2,0:T(4,128)S(1)} %fusion.150, s32[128]{0:T(128)S(1)} %iota_add_fusion.2, s32[128,64]{0,1:T(8,128)S(1)} %get-tuple-element.440, bf16[1,4,128,128]{2,1,3,0:T(4,128)(2,1)S(1)} %copy.2824), kind=kOutput, calls=%fused_computation.15.clone.1 | convolution fusion | flops 25198592 | bytes 426496 | tf_op jit(solution)/shard_map/while/body/eval_jaxpr/bck,cdk->dbk/dot_general | solution.py:69
  521.0 16.7 %fusion.148 = f32[128,64,4]{1,2,0:T(4,128)S(1)} fusion(s32[128]{0:T(128)S(1)} %iota_add_fusion.2, s32[128,64]{0,1:T(8,128)S(1)} %get-tuple-element.440, bf16[1,4,128,128]{2,1,3,0:T(4,128)(2,1)S(1)} %copy.2824), kind=kOutput, calls=%fused_computation.10.clone.1 | convolution fusion | flops 24117248 | bytes 295424 | tf_op jit(solution)/shard_map/while/body/eval_jaxpr/bck,cdk->dbk/dot_general | solution.py:72
  537.7 17.0 %fusion.149 = f32[64,1,4,128]{0,2,3,1:T(4,128)S(1)} fusion(f32[128,64,4]{1,2,0:T(4,128)S(1)} %fusion.148, s32[128]{0:T(128)S(1)} %iota_add_fusion.2, s32[128,64]{0,1:T(8,128)S(1)} %get-tuple-element.440, bf16[1,4,128,128]{2,1,3,0:T(4,128)(2,1)S(1)} %copy.2825), kind=kOutput, calls=%fused_computation.17.clone.1 | convolution fusion | flops 25198592 | bytes 426496 | tf_op jit(solution)/shard_map/while/body/eval_jaxpr/bck,cdk->dbk/dot_general | solution.py:70
  555.2 275.3 %all-reduce.2 = bf16[64,2,4,1024]{3,2,1,0:T(4,128)(2,1)S(1)} all-reduce(f32[64,2,4,1024]{3,2,1,0:T(4,128)S(1)} %get-tuple-element.138), channel_id=2, replica_groups=mesh['chan'=8,'dm'=8,'bin'=4] {'chan','dm'}, use_global_device_ids=true, to_apply=%region_2.3.clone | all-reduce | flops 524288 | bytes 3145728
  (154 shorter events, 61.6 us)
Async XLA Ops:
  0.0 0.8 copy-start.1
  555.2 275.4 %copy-start.2 = (u32[256]{0:T(256)S(1)}, u32[256]{0:T(256)}, u32[]{:S(2)}) copy-start(u32[256]{0:T(256)} %constant.93) | copy-start | bytes 3076
  555.2 282.7 %copy-start = (bf16[2,64,64]{2,1,0:T(8,128)(2,1)S(1)}, bf16[2,64,64]{2,1,0:T(8,128)(2,1)}, u32[]{:S(2)}) copy-start(bf16[2,64,64]{2,1,0:T(8,128)(2,1)} %param.7) | copy-start | bytes 49156
  831.9 6.3 collective-permute-start
  833.2 6.3 collective-permute-start.1
where the time goes:
time: 846 us; the launch traced here: 844 us
  matrix products  541 us (64%)
  blocking collectives  275 us (33%)
  local copies, waits for them, and re-layouts  17.6 us (2%)
    unnamed x1, blocking collectives  275 us
    dot_general x8, matrix products, one_block(): jnp.einsum('bck,cdk->dbk', piece[1], phase_im, preferred_element_type=jnp...  136 us
    dot_general x8, matrix products, one_block(): jnp.einsum('bck,cdk->dbk', piece[0], phase_im, preferred_element_type=jnp...  136 us
    dot_general x8, matrix products, one_block(): jnp.einsum('bck,cdk->dbk', piece[0], phase_re, preferred_element_type=jnp...  134 us
    dot_general x8, matrix products, one_block(): jnp.einsum('bck,cdk->dbk', piece[1], phase_re, preferred_element_type=jnp...  134 us
  transfers between devices with their start and end apart: 2, of which 0 were waited for; matrix products, arithmetic and copies ran while one was open for 0% of the time, Pallas kernels for 0%

commit v1 on v0

v1 whole, which is shorter than its diff:
```python
import math
from functools import partial

import jax
import jax.numpy as jnp
from jax import lax
from jax.experimental import pallas as pl
from jax.experimental.pallas import tpu as pltpu
from jax.sharding import PartitionSpec as P

D = 64
BEAMS = 4
TEMPLATES = 64
TAPS = 64
GROUP = 16
TILE = 128
SUB = TILE // GROUP
LANES = 2 * BEAMS
PHASE_DT = jnp.bfloat16
F32 = jnp.float32
BF16 = jnp.bfloat16


def swap_blocks(tiles):
    tiles = list(tiles)
    lane = lax.broadcasted_iota(jnp.int32, tiles[0].shape, 1)
    for step in (4, 2, 1):
        upper = (lane // GROUP) & step != 0
        fresh = list(tiles)
        for low in range(SUB):
            if low & step == 0:
                high = low | step
                fresh[low] = jnp.where(upper, pltpu.roll(tiles[high], step * GROUP, 1), tiles[low])
                fresh[high] = jnp.where(
                    upper, tiles[high], pltpu.roll(tiles[low], TILE - step * GROUP, 1)
                )
        tiles = fresh
    return tiles


def unit(count, period):
    rest = count & (period - 1)
    rest = jnp.where(rest >= period // 2, rest - period, rest)
    angle = rest.astype(F32) * (2.0 * math.pi / period)
    return jnp.cos(angle), jnp.sin(angle)


def times(a, b):
    return a[0] * b[0] - a[1] * b[1], a[0] * b[1] + a[1] * b[0]


def channel_sums(first_ref, delay_ref, x_ref, out_ref, fine_ref, mid_ref, base_ref, w_ref, *, period):
    tile = pl.program_id(0)
    half = GROUP // 2

    @pl.when(tile == 0)
    def _():
        n = delay_ref[...].T
        one = unit(n, period)
        group = unit(n * GROUP, period)
        wide = unit(n * TILE, period)
        start = unit(n * first_ref[0], period)
        power = one
        for j in range(1, half + 1):
            fine_ref[0, j] = power[0].astype(PHASE_DT)
            fine_ref[1, j] = power[1].astype(PHASE_DT)
            if j == half:
                mid = power
            power = times(power, one)
        for g in range(SUB):
            mid_ref[0, g] = mid[0]
            mid_ref[1, g] = mid[1]
            mid = times(mid, group)
        base_ref[0] = start[0]
        base_ref[1] = start[1]
        base_ref[2] = wide[0]
        base_ref[3] = wide[1]

    @pl.when(tile > 0)
    def _():
        moved = times((base_ref[0], base_ref[1]), (base_ref[2], base_ref[3]))
        base_ref[0] = moved[0]
        base_ref[1] = moved[1]

    lanes = lax.broadcasted_iota(jnp.int32, (128, TILE), 1)
    native = [x_ref[j // BEAMS, j % BEAMS].astype(F32) for j in range(LANES)]
    for g, mixed in enumerate(swap_blocks(native)):
        w_ref[g, 0:128, :] = mixed.astype(BF16)
        turned = pltpu.roll(mixed, TILE // 2, 1)
        w_ref[g, 128:256, :] = jnp.where(lanes >= TILE // 2, -turned, turned).astype(BF16)

    bin_of_lane = lax.broadcasted_iota(jnp.int32, (D, TILE), 1) & (GROUP - 1)

    def one_group(g):
        turn = times((base_ref[0], base_ref[1]), (mid_ref[0, g], mid_ref[1, g]))
        fc = turn[0].astype(PHASE_DT)
        fs = turn[1].astype(PHASE_DT)
        rows = [None] * GROUP
        rows[half] = (fc, fs)
        for j in range(1, half + 1):
            ec = fine_ref[0, j]
            es = fine_ref[1, j]
            cc = fc * ec
            ss = fs * es
            sc = fs * ec
            cs = fc * es
            if j < half:
                rows[half + j] = (cc - ss, sc + cs)
            rows[half - j] = (cc + ss, sc - cs)
        left = jnp.concatenate(
            [jnp.concatenate([c.astype(BF16), s.astype(BF16)], axis=1) for c, s in rows], axis=0
        )
        prod = jnp.dot(left, w_ref[g], preferred_element_type=F32)
        acc = prod[0:D]
        for k in range(1, GROUP):
            acc = jnp.where(bin_of_lane == k, prod[k * D : (k + 1) * D], acc)
        return acc.reshape(D // 8, 8, TILE)

    for pair in range(SUB // 2):
        both = jnp.concatenate([one_group(2 * pair), one_group(2 * pair + 1)], axis=1)
        out_ref[:, pl.ds(pair * 16, 16), :] = both.astype(BF16)


def dedisperse(spectra, delays, first, period):
    width = spectra.shape[3]
    tiles = width // TILE
    rows = width // GROUP * 8
    return pl.pallas_call(
        partial(channel_sums, period=period),
        grid_spec=pltpu.PrefetchScalarGridSpec(
            num_scalar_prefetch=1,
            grid=(tiles,),
            in_specs=[
                pl.BlockSpec((128, D), lambda i, s: (0, 0)),
                pl.BlockSpec((2, BEAMS, 128, TILE), lambda i, s: (0, 0, 0, i)),
            ],
            out_specs=pl.BlockSpec((D // 8, SUB * 8, TILE), lambda i, s: (0, i, 0)),
            scratch_shapes=[
                pltpu.VMEM((2, GROUP // 2 + 1, D, 128), PHASE_DT),
                pltpu.VMEM((2, SUB, D, 128), F32),
                pltpu.VMEM((4, D, 128), F32),
                pltpu.VMEM((SUB, 256, TILE), BF16),
            ],
        ),
        out_shape=jax.ShapeDtypeStruct((D // 8, rows, TILE), BF16),
        name="channel_sums",
    )(first, delays, spectra)


def fold_kernel(x_ref, out_ref, sum_ref):
    total = x_ref[0].astype(F32)
    for i in range(1, x_ref.shape[0]):
        total = total + x_ref[i].astype(F32)
    sum_ref[...] = total
    for d in range(8):
        out_ref[d] = sum_ref[pl.ds(d, total.shape[0] // 8, stride=8), :].astype(BF16)


def fold(received):
    count, rows, lanes = received.shape
    return pl.pallas_call(
        fold_kernel,
        out_shape=jax.ShapeDtypeStruct((8, rows // 8, lanes), BF16),
        scratch_shapes=[pltpu.VMEM((rows, lanes), F32)],
        name="fold",
    )(received)


def finish_kernel(x_ref, out_ref, *, scale):
    total = x_ref[0].astype(F32)
    for i in range(1, x_ref.shape[0]):
        total = total + x_ref[i].astype(F32)
    out_ref[...] = (total * scale).astype(BF16)


def finish(received, scale):
    return pl.pallas_call(
        partial(finish_kernel, scale=scale),
        out_shape=jax.ShapeDtypeStruct(received.shape[1:], BF16),
        name="finish",
    )(received)


def response_kernel(y_ref, left_ref, right_ref, h_ref, out_ref, u_ref, win_ref, pow_ref):
    rows = y_ref.shape[0]
    edge = left_ref.shape[0]
    tiles = rows // SUB
    u_ref[...] = jnp.zeros(u_ref.shape, F32)
    u_ref[0:edge, :] = left_ref[...].astype(F32)
    u_ref[pl.ds(edge, rows), :] = y_ref[...].astype(F32)
    u_ref[pl.ds(edge + rows, edge), :] = right_ref[...].astype(F32)
    blocks = [u_ref[pl.ds(g, 16, stride=SUB), :] for g in range(SUB)]
    series = swap_blocks(blocks)
    for j in range(LANES):
        ri, beam = divmod(j, BEAMS)
        for m in range(tiles):
            wide = jnp.concatenate([series[j][m : m + 1], series[j][m + 1 : m + 2]], axis=1)
            wide = jnp.broadcast_to(wide, (TAPS, 2 * TILE))
            turned = pltpu.roll(wide, 2 * TILE - (TAPS - 1), 1, stride=1, stride_axis=0)
            win_ref[beam, pl.ds(ri * TAPS, TAPS), pl.ds(m * TILE, TILE)] = turned[:, :TILE].astype(BF16)
    row = lax.broadcasted_iota(jnp.int32, (TAPS, TAPS), 0)
    col = lax.broadcasted_iota(jnp.int32, (TAPS, TAPS), 1)
    flip = jnp.where(row + col == TAPS - 1, 1.0, 0.0).astype(BF16)
    h_re = jnp.dot(h_ref[0], flip, preferred_element_type=F32)
    h_im = jnp.dot(h_ref[1], flip, preferred_element_type=F32)
    weights = jnp.concatenate(
        [jnp.concatenate([h_re, -h_im], axis=1), jnp.concatenate([h_im, h_re], axis=1)], axis=0
    ).astype(BF16)
    for beam in range(BEAMS):
        resp = jnp.dot(weights, win_ref[beam], preferred_element_type=F32)
        re = resp[:TEMPLATES]
        im = resp[TEMPLATES:]
        power = re * re + im * im
        for m in range(tiles):
            pow_ref[pl.ds(m * TEMPLATES * BEAMS + beam, TEMPLATES, stride=BEAMS), :] = power[:, m * TILE : (m + 1) * TILE]
    for m in range(tiles):
        part = pow_ref[pl.ds(m * TEMPLATES * BEAMS, TEMPLATES * BEAMS), :]
        out_ref[0, :, :, pl.ds(m * TILE, TILE)] = part.reshape(TEMPLATES, BEAMS, TILE).astype(BF16)


def response(y, left, right, templates):
    rows = y.shape[0]
    width = rows * GROUP
    return pl.pallas_call(
        response_kernel,
        out_shape=jax.ShapeDtypeStruct((1, TEMPLATES, BEAMS, width), BF16),
        scratch_shapes=[
            pltpu.VMEM((16 * SUB, TILE), F32),
            pltpu.VMEM((BEAMS, 2 * TAPS, width), BF16),
            pltpu.VMEM((TEMPLATES * BEAMS * width // TILE, TILE), F32),
        ],
        name="response",
    )(y, left, right, templates)


def shards(spectra, delays, templates):
    width = spectra.shape[3]
    period = 2 * width * lax.axis_size("bin")
    scale = 1.0 / math.sqrt(spectra.shape[2] * lax.axis_size(("chan", "dm")))
    first = (lax.axis_index("bin") * width).reshape(1).astype(jnp.int32)
    partial_sums = dedisperse(spectra, delays, first, period)
    received = lax.all_to_all(partial_sums, "chan", 0, 0, tiled=True)
    received = lax.all_to_all(fold(received), "dm", 0, 0, tiled=True)
    y = finish(received, scale)
    edge = TAPS // 2 // GROUP
    count = lax.axis_size("bin")
    up = [(i, i + 1) for i in range(count - 1)]
    down = [(i + 1, i) for i in range(count - 1)]
    left = lax.ppermute(y[y.shape[0] - edge :], "bin", up)
    right = lax.ppermute(y[:edge], "bin", down)
    return response(y, left, right, templates)


def solution(mesh):
    placed = (P(None, None, ("chan", "dm"), "bin"), P(("chan", "dm"), None), P())
    return jax.shard_map(
        shards,
        mesh=mesh,
        in_specs=placed,
        out_specs=P(("chan", "dm"), None, None, "bin"),
        check_vma=False,
    )
```

time: 846 us -> 71.5 us (0.08)
  matrix products: 541 us -> 0 us
  blocking collectives: 275 us -> 38.2 us
  Pallas kernels: 0 us -> 21.9 us
  local copies, waits for them, and re-layouts: 17.6 us -> 2.68 us
    dot_general x33 -> x0, matrix products: 541 us -> none  [the longest x8 136 us: one_block(): jnp.einsum('bck,cdk->dbk', piece[1], phase_im, preferred_element_type=jnp...]
    unnamed x1 -> x0, blocking collectives: 275 us -> none
    all_to_all x0 -> x2, blocking collectives: none -> 38.2 us  [the longest x1 20.5 us: shards(): received = lax.all_to_all(partial_sums, 'chan', 0, 0, tiled=True)]
    pallas_call x0 -> x4, Pallas kernels: none -> 21.9 us  [the longest x1 15.5 us: dedisperse(): pl.pallas_call(partial(channel_sums, period=period), grid_spec=pltpu.Pref...]
  transfers between devices with their start and end apart: 2 -> 2, of which waited for: 0 -> 1; matrix products, arithmetic and copies ran while one was open for 0% -> 0% of each run, Pallas kernels for 0% -> 0%
where the time goes in v1:
time: 71.5 us; the launch traced here: 71 us
  blocking collectives  38.2 us (53%)
  Pallas kernels  21.9 us (31%)
  waiting for transfers between devices  4.14 us (6%)
  starting transfers between devices  4.01 us (6%)
  local copies, waits for them, and re-layouts  2.68 us (4%)
    all_to_all x1, blocking collectives, shards(): received = lax.all_to_all(partial_sums, 'chan', 0, 0, tiled=True)  20.5 us
    all_to_all x1, blocking collectives, shards(): received = lax.all_to_all(fold(received), 'dm', 0, 0, tiled=True)  17.6 us
    pallas_call x1, Pallas kernels, dedisperse(): pl.pallas_call(partial(channel_sums, period=period), grid_spec=pltpu.Pref...  15.5 us
    ppermute x1, waiting for transfers between devices, shards(): left = lax.ppermute(y[y.shape[0] - edge:], 'bin', up)  4.14 us
    pallas_call x1, Pallas kernels, response(): pl.pallas_call(response_kernel, out_shape=jax.ShapeDtypeStruct((1, TEMPLA...  2.82 us
    ppermute x1, starting transfers between devices, shards(): right = lax.ppermute(y[:edge], 'bin', down)  2.72 us
    pallas_call x1, Pallas kernels, fold(): pl.pallas_call(fold_kernel, out_shape=jax.ShapeDtypeStruct((8, rows // 8,...  2.09 us
    unnamed x5, local copies, waits for them, and re-layouts  2.01 us
  transfers between devices with their start and end apart: 2, of which 1 were waited for; matrix products, arithmetic and copies ran while one was open for 0% of the time, Pallas kernels for 0%

profile of v1, /device:TPU:6, one launch (start us, length us, event | category | flops | bytes accessed | tf_op | source)
XLA Modules:
  0.0 71.0 jit_solution(9469606523010105221)
XLA Ops:
  0.0 1.5 %copy.4.delay_ref = s32[128,64]{1,0:T(8,128)} copy(s32[128,64]{0,1:T(8,128)} %param.4) | data formatting | bytes 65536 | tf_op args[1]
  1.5 15.5 %channel_sums.1 = bf16[8,512,128]{2,1,0:T(8,128)(2,1)} custom-call(s32[1]{0:T(128)} %bitcast.first_ref, s32[128,64]{1,0:T(8,128)} %copy.4.delay_ref, bf16[2,4,128,1024]{3,2,1,0:T(8,128)(2,1)} %x_ref.1), custom_call_target="tpu_custom_call" | custom-call | tf_op jit(solution)/shard_map/channel_sums/pallas_call | solution.py:128
  17.0 20.5 %all_to_all.10.x_ref = bf16[8,512,128]{2,1,0:T(8,128)(2,1)} all-to-all(bf16[8,512,128]{2,1,0:T(8,128)(2,1)} %channel_sums.1), channel_id=1, replica_groups=mesh['chan'=8,'dm'=8,'bin'=4] {'chan'}, dimensions={0} | all-to-all | bytes 2097152 | tf_op jit(solution)/shard_map/all_to_all | solution.py:242
  37.5 2.1 %fold.1 = bf16[8,64,128]{2,1,0:T(8,128)(2,1)} custom-call(bf16[8,512,128]{2,1,0:T(8,128)(2,1)} %all_to_all.10.x_ref), custom_call_target="tpu_custom_call" | custom-call | tf_op jit(solution)/shard_map/fold/pallas_call | solution.py:161
  39.6 17.6 %all_to_all.11.x_ref = bf16[8,64,128]{2,1,0:T(8,128)(2,1)} all-to-all(bf16[8,64,128]{2,1,0:T(8,128)(2,1)} %fold.1), channel_id=1, replica_groups=mesh['chan'=8,'dm'=8,'bin'=4] {'dm'}, dimensions={0} | all-to-all | bytes 262144 | tf_op jit(solution)/shard_map/all_to_all | solution.py:243
  57.2 1.5 %finish.1.y_ref = bf16[64,128]{1,0:T(8,128)(2,1)} custom-call(bf16[8,64,128]{2,1,0:T(8,128)(2,1)} %all_to_all.11.x_ref), custom_call_target="tpu_custom_call" | custom-call | tf_op jit(solution)/shard_map/finish/pallas_call | solution.py:177
  58.8 0.7 fusion
  59.4 2.7 %collective-permute-start.1 = (bf16[2,128]{1,0:T(2,128)(2,1)S(1)}, bf16[2,128]{1,0:T(2,128)(2,1)S(1)}, u32[]{:S(2)}, u32[]{:S(2)}) collective-permute-start(bf16[2,128]{1,0:T(2,128)(2,1)S(1)} %get-tuple-element.5), channel_id=1, source_target_pairs={{1,0},{2,1},{3,2},{5,4},{6,5},{7,6},{9,8},{10,9},{11,10},{13,12},{... | collective-permute-start | bytes 1544 | tf_op jit(solution)/shard_map/ppermute | solution.py:250
  62.2 1.3 %collective-permute-start = (bf16[2,128]{1,0:T(2,128)(2,1)S(1)}, bf16[2,128]{1,0:T(2,128)(2,1)S(1)}, u32[]{:S(2)}, u32[]{:S(2)}) collective-permute-start(bf16[2,128]{1,0:T(2,128)(2,1)S(1)} %get-tuple-element.6), channel_id=1, source_target_pairs={{0,1},{1,2},{2,3},{4,5},{5,6},{6,7},{8,9},{9,10},{10,11},{12,13},{... | collective-permute-start | bytes 1544 | tf_op jit(solution)/shard_map/ppermute | solution.py:249
  63.5 0.0 collective-permute-done.1.right_ref
  63.5 0.0 copy-start
  63.5 4.1 %collective-permute-done.left_ref = bf16[2,128]{1,0:T(2,128)(2,1)S(1)} collective-permute-done((bf16[2,128]{1,0:T(2,128)(2,1)S(1)}, bf16[2,128]{1,0:T(2,128)(2,1)S(1)}, u32[]{:S(2)}, u32[]{:S(2)}) %collective-permute-start) | collective-permute-done | bytes 544 | tf_op jit(solution)/shard_map/ppermute | solution.py:249
  67.6 0.0 copy-done
  67.6 0.0 copy-start.1
  67.6 0.5 copy-done.1
  68.1 2.8 %response.1 = bf16[1,64,4,1024]{3,2,1,0:T(4,128)(2,1)} custom-call(bf16[64,128]{1,0:T(8,128)(2,1)} %finish.1.y_ref, bf16[2,128]{1,0:T(2,128)(2,1)} %copy-done.1, bf16[2,128]{1,0:T(2,128)(2,1)} %copy-done, bf16[2,64,64]{2,1,0:T(8,128)(2,1)} %h_ref.1), custom_call_target="tpu_custom_call" | custom-call | tf_op jit(solution)/shard_map/response/pallas_call | solution.py:224
Async XLA Ops:
  59.4 4.0 %collective-permute-start.1 = (bf16[2,128]{1,0:T(2,128)(2,1)S(1)}, bf16[2,128]{1,0:T(2,128)(2,1)S(1)}, u32[]{:S(2)}, u32[]{:S(2)}) collective-permute-start(bf16[2,128]{1,0:T(2,128)(2,1)S(1)} %get-tuple-element.5), channel_id=1, source_target_pairs={{1,0},{2,1},{3,2},{5,4},{6,5},{7,6},{9,8},{10,9},{11,10},{13,12},{... | collective-permute-start | bytes 1544 | tf_op jit(solution)/shard_map/ppermute | solution.py:250
  62.2 5.5 %collective-permute-start = (bf16[2,128]{1,0:T(2,128)(2,1)S(1)}, bf16[2,128]{1,0:T(2,128)(2,1)S(1)}, u32[]{:S(2)}, u32[]{:S(2)}) collective-permute-start(bf16[2,128]{1,0:T(2,128)(2,1)S(1)} %get-tuple-element.6), channel_id=1, source_target_pairs={{0,1},{1,2},{2,3},{4,5},{5,6},{6,7},{8,9},{9,10},{10,11},{12,13},{... | collective-permute-start | bytes 1544 | tf_op jit(solution)/shard_map/ppermute | solution.py:249
  63.5 4.2 %copy-start = (bf16[2,128]{1,0:T(2,128)(2,1)}, bf16[2,128]{1,0:T(2,128)(2,1)S(1)}, u32[]{:S(2)}) copy-start(bf16[2,128]{1,0:T(2,128)(2,1)S(1)} %collective-permute-done.1.right_ref) | copy-start | bytes 1540
  67.6 0.5 copy-start.1

commit v2 on v1

v2 whole, which is shorter than its diff:
```python
import math
from functools import partial

import jax
import jax.numpy as jnp
from jax import lax
from jax.experimental import pallas as pl
from jax.experimental.pallas import tpu as pltpu
from jax.sharding import PartitionSpec as P

D = 64
BEAMS = 4
TEMPLATES = 64
TAPS = 64
GROUP = 16
TILE = 128
SUB = TILE // GROUP
LANES = 2 * BEAMS
PER_HOP = 16
PHASE_DT = jnp.bfloat16
F32 = jnp.float32
BF16 = jnp.bfloat16


def swap_blocks(tiles):
    tiles = list(tiles)
    lane = lax.broadcasted_iota(jnp.int32, tiles[0].shape, 1)
    for step in (4, 2, 1):
        upper = (lane // GROUP) & step != 0
        fresh = list(tiles)
        for low in range(SUB):
            if low & step == 0:
                high = low | step
                fresh[low] = jnp.where(upper, pltpu.roll(tiles[high], step * GROUP, 1), tiles[low])
                fresh[high] = jnp.where(
                    upper, tiles[high], pltpu.roll(tiles[low], TILE - step * GROUP, 1)
                )
        tiles = fresh
    return tiles


def unit(count, period):
    rest = count & (period - 1)
    rest = jnp.where(rest >= period // 2, rest - period, rest)
    angle = rest.astype(F32) * (2.0 * math.pi / period)
    return jnp.cos(angle), jnp.sin(angle)


def times(a, b):
    return a[0] * b[0] - a[1] * b[1], a[0] * b[1] + a[1] * b[0]


def near(x):
    return pltpu.with_memory_space_constraint(x, pltpu.VMEM)


def channel_sums(place_ref, delay_ref, x_ref, *rest, period, offsets, hops, build):
    out_refs, rest = rest[: len(offsets)], rest[len(offsets) :]
    if build:
        w_ref, fine_ref, mid_ref, base_ref = rest
    else:
        w_ref = x_ref
        fine_ref, mid_ref, base_ref = rest
    tile = pl.program_id(0)
    half = GROUP // 2
    count = len(offsets) * PER_HOP

    @pl.when(tile == 0)
    def _():
        n = jnp.concatenate(
            [
                delay_ref[pl.ds(pl.multiple_of((place_ref[1] + s) % hops * PER_HOP, PER_HOP), PER_HOP), :]
                for s in offsets
            ],
            axis=0,
        )
        one = unit(n, period)
        group = unit(n * GROUP, period)
        wide = unit(n * TILE, period)
        start = unit(n * place_ref[0], period)
        power = one
        for j in range(1, half + 1):
            fine_ref[0, j] = power[0].astype(PHASE_DT)
            fine_ref[1, j] = power[1].astype(PHASE_DT)
            if j == half:
                mid = power
            power = times(power, one)
        for g in range(SUB):
            mid_ref[0, g] = mid[0]
            mid_ref[1, g] = mid[1]
            mid = times(mid, group)
        base_ref[0] = start[0]
        base_ref[1] = start[1]
        base_ref[2] = wide[0]
        base_ref[3] = wide[1]

    @pl.when(tile > 0)
    def _():
        moved = times((base_ref[0], base_ref[1]), (base_ref[2], base_ref[3]))
        base_ref[0] = moved[0]
        base_ref[1] = moved[1]

    if build:
        lanes = lax.broadcasted_iota(jnp.int32, (128, TILE), 1)
        native = [x_ref[j // BEAMS, j % BEAMS].astype(F32) for j in range(LANES)]
        for g, mixed in enumerate(swap_blocks(native)):
            w_ref[tile * SUB + g, 0:128, :] = mixed.astype(BF16)
            turned = pltpu.roll(mixed, TILE // 2, 1)
            w_ref[tile * SUB + g, 128:256, :] = jnp.where(lanes >= TILE // 2, -turned, turned).astype(BF16)

    bin_of_lane = lax.broadcasted_iota(jnp.int32, (count, TILE), 1) & (GROUP - 1)

    def one_group(g):
        turn = times((base_ref[0], base_ref[1]), (mid_ref[0, g], mid_ref[1, g]))
        fc = turn[0].astype(PHASE_DT)
        fs = turn[1].astype(PHASE_DT)
        rows = [None] * GROUP
        rows[half] = (fc, fs)
        for j in range(1, half + 1):
            ec = fine_ref[0, j]
            es = fine_ref[1, j]
            cc = fc * ec
            ss = fs * es
            sc = fs * ec
            cs = fc * es
            if j < half:
                rows[half + j] = (cc - ss, sc + cs)
            rows[half - j] = (cc + ss, sc - cs)
        left = jnp.concatenate(
            [jnp.concatenate([c.astype(BF16), s.astype(BF16)], axis=1) for c, s in rows], axis=0
        )
        prod = jnp.dot(left, w_ref[tile * SUB + g], preferred_element_type=F32)
        acc = prod[0:count]
        for k in range(1, GROUP):
            acc = jnp.where(bin_of_lane == k, prod[k * count : (k + 1) * count], acc)
        return acc.reshape(count // 8, 8, TILE)

    for pair in range(SUB // 2):
        both = jnp.concatenate([one_group(2 * pair), one_group(2 * pair + 1)], axis=1)
        part = PER_HOP // 8
        for i, out_ref in enumerate(out_refs):
            out_ref[:, pl.ds(pl.multiple_of(tile * SUB * 8 + pair * 16, 16), 16), :] = both[i * part : (i + 1) * part].astype(out_ref.dtype)


def dedisperse(x, delays, place, period, offsets, hops, build, dtype):
    tiles = x.shape[3] // TILE if build else x.shape[0] // SUB
    count = len(offsets) * PER_HOP
    x_spec = pl.BlockSpec((2, BEAMS, 128, TILE), lambda i, s: (0, 0, 0, i))
    w_spec = pl.BlockSpec(memory_space=pltpu.VMEM)
    part = PER_HOP // 8
    out_specs = [pl.BlockSpec(memory_space=pltpu.VMEM)] * len(offsets)
    out_shapes = [pltpu.VMEM((part, tiles * SUB * 8, TILE), dtype)] * len(offsets)
    w_shape = pltpu.VMEM((tiles * SUB, 256, TILE), BF16)
    return pl.pallas_call(
        partial(channel_sums, period=period, offsets=offsets, hops=hops, build=build),
        grid_spec=pltpu.PrefetchScalarGridSpec(
            num_scalar_prefetch=1,
            grid=(tiles,),
            in_specs=[
                pl.BlockSpec((D, 128), lambda i, s: (0, 0)),
                x_spec if build else w_spec,
            ],
            out_specs=out_specs + [w_spec] * build,
            scratch_shapes=[
                pltpu.VMEM((2, GROUP // 2 + 1, count, 128), PHASE_DT),
                pltpu.VMEM((2, SUB, count, 128), F32),
                pltpu.VMEM((4, count, 128), F32),
            ],
        ),
        out_shape=out_shapes + [w_shape] * build,
        compiler_params=pltpu.CompilerParams(vmem_limit_bytes=24 * 2**20),
        name="channel_sums",
    )(place, delays, x if build else near(x))


def fold_kernel(own_ref, far_ref, up_ref, down_ref, out_ref, sum_ref):
    for core in range(own_ref.shape[0]):
        total = own_ref[core].astype(F32)
        for ref in (far_ref, up_ref, down_ref):
            total = total + ref[core].astype(F32)
        sum_ref[...] = total
        for d in range(8):
            out_ref[core * 8 + d] = sum_ref[pl.ds(d, total.shape[0] // 8, stride=8), :].astype(BF16)


def fold(own, far, up, down):
    cores, rows, lanes = own.shape
    return pl.pallas_call(
        fold_kernel,
        in_specs=[pl.BlockSpec(memory_space=pltpu.VMEM)] * 4,
        out_specs=pl.BlockSpec(memory_space=pltpu.VMEM),
        out_shape=pltpu.VMEM((cores * 8, rows // 8, lanes), BF16),
        scratch_shapes=[pltpu.VMEM((rows, lanes), F32)],
        compiler_params=pltpu.CompilerParams(vmem_limit_bytes=24 * 2**20),
        name="fold",
    )(near(own), near(far), near(up), near(down))


def finish_kernel(x_ref, out_ref, head_ref, tail_ref, *, scale):
    total = x_ref[0].astype(F32)
    for i in range(1, x_ref.shape[0]):
        total = total + x_ref[i].astype(F32)
    y = (total * scale).astype(BF16)
    edge = head_ref.shape[0]
    out_ref[...] = y
    head_ref[...] = y[:edge]
    tail_ref[...] = y[y.shape[0] - edge :]


def finish(received, scale, edge):
    rows, lanes = received.shape[1:]
    return pl.pallas_call(
        partial(finish_kernel, scale=scale),
        in_specs=[pl.BlockSpec(memory_space=pltpu.VMEM)] * 1,
        out_specs=[pl.BlockSpec(memory_space=pltpu.VMEM)] * 3,
        out_shape=[pltpu.VMEM((n, lanes), BF16) for n in (rows, edge, edge)],
        compiler_params=pltpu.CompilerParams(vmem_limit_bytes=24 * 2**20),
        name="finish",
    )(near(received))


def response_kernel(place_ref, y_ref, left_ref, right_ref, h_ref, out_ref, u_ref, win_ref, pow_ref):
    rows = y_ref.shape[0]
    edge = left_ref.shape[0]
    tiles = rows // SUB
    u_ref[...] = jnp.zeros(u_ref.shape, F32)
    u_ref[0:edge, :] = jnp.where(place_ref[0] > 0, left_ref[...].astype(F32), 0.0)
    u_ref[pl.ds(edge, rows), :] = y_ref[...].astype(F32)
    u_ref[pl.ds(edge + rows, edge), :] = jnp.where(place_ref[2] > 0, right_ref[...].astype(F32), 0.0)
    blocks = [u_ref[pl.ds(g, 16, stride=SUB), :] for g in range(SUB)]
    series = swap_blocks(blocks)
    for j in range(LANES):
        ri, beam = divmod(j, BEAMS)
        for m in range(tiles):
            wide = jnp.concatenate([series[j][m : m + 1], series[j][m + 1 : m + 2]], axis=1)
            wide = jnp.broadcast_to(wide, (TAPS, 2 * TILE))
            turned = pltpu.roll(wide, 2 * TILE - (TAPS - 1), 1, stride=1, stride_axis=0)
            win_ref[beam, pl.ds(ri * TAPS, TAPS), pl.ds(m * TILE, TILE)] = turned[:, :TILE].astype(BF16)
    row = lax.broadcasted_iota(jnp.int32, (TAPS, TAPS), 0)
    col = lax.broadcasted_iota(jnp.int32, (TAPS, TAPS), 1)
    flip = jnp.where(row + col == TAPS - 1, 1.0, 0.0).astype(BF16)
    h_re = jnp.dot(h_ref[0], flip, preferred_element_type=F32)
    h_im = jnp.dot(h_ref[1], flip, preferred_element_type=F32)
    weights = jnp.concatenate(
        [jnp.concatenate([h_re, -h_im], axis=1), jnp.concatenate([h_im, h_re], axis=1)], axis=0
    ).astype(BF16)
    for beam in range(BEAMS):
        resp = jnp.dot(weights, win_ref[beam], preferred_element_type=F32)
        re = resp[:TEMPLATES]
        im = resp[TEMPLATES:]
        power = re * re + im * im
        for m in range(tiles):
            pow_ref[pl.ds(m * TEMPLATES * BEAMS + beam, TEMPLATES, stride=BEAMS), :] = power[:, m * TILE : (m + 1) * TILE]
    for m in range(tiles):
        part = pow_ref[pl.ds(m * TEMPLATES * BEAMS, TEMPLATES * BEAMS), :]
        out_ref[0, :, :, pl.ds(m * TILE, TILE)] = part.reshape(TEMPLATES, BEAMS, TILE).astype(BF16)


def response(place, y, left, right, templates):
    rows = y.shape[0]
    width = rows * GROUP
    return pl.pallas_call(
        response_kernel,
        grid_spec=pltpu.PrefetchScalarGridSpec(
            num_scalar_prefetch=1,
            in_specs=[pl.BlockSpec(memory_space=pltpu.VMEM)] * 4,
            scratch_shapes=[
                pltpu.VMEM((16 * SUB, TILE), F32),
                pltpu.VMEM((BEAMS, 2 * TAPS, width), BF16),
                pltpu.VMEM((TEMPLATES * BEAMS * width // TILE, TILE), F32),
            ],
        ),
        out_shape=jax.ShapeDtypeStruct((1, TEMPLATES, BEAMS, width), BF16),
        compiler_params=pltpu.CompilerParams(vmem_limit_bytes=24 * 2**20),
        name="response",
    )(place, near(y), near(left), near(right), templates)


def shards(spectra, delays, templates):
    width = spectra.shape[3]
    bins = lax.axis_size("bin")
    chans = lax.axis_size("chan")
    dms = lax.axis_size("dm")
    period = 2 * width * bins
    scale = 1.0 / math.sqrt(spectra.shape[2] * chans * dms)
    cores = PER_HOP // 8
    hops = chans // cores
    place = jnp.stack(
        [
            lax.axis_index("bin") * width,
            lax.axis_index("chan") // cores,
            bins - 1 - lax.axis_index("bin"),
        ]
    ).astype(jnp.int32)
    table = delays.T

    def moved(x, s):
        return lax.ppermute(x, "chan", [(i, (i + s * cores) % chans) for i in range(chans)])

    far, weights = dedisperse(spectra, table, place, period, (2,), hops, True, BF16)
    far = moved(far, 2)
    up, down = dedisperse(weights, table, place, period, (1, 3), hops, False, BF16)
    up = moved(up, 1)
    down = moved(down, 3)
    (own,) = dedisperse(weights, table, place, period, (0,), hops, False, F32)
    groups = [
        [(hop * cores + core) * dms + dm for core in range(cores) for dm in range(dms)]
        for hop in range(hops)
    ]
    received = lax.all_to_all(
        fold(own, far, up, down), ("chan", "dm"), 0, 0, axis_index_groups=groups, tiled=True
    )
    edge = TAPS // 2 // GROUP
    y, head, tail = finish(received, scale, edge)
    left = lax.ppermute(tail, "bin", [(i, (i + 1) % bins) for i in range(bins)])
    right = lax.ppermute(head, "bin", [((i + 1) % bins, i) for i in range(bins)])
    return response(place, y, left, right, templates)


def solution(mesh):
    placed = (P(None, None, ("chan", "dm"), "bin"), P(("chan", "dm"), None), P())
    return jax.shard_map(
        shards,
        mesh=mesh,
        in_specs=placed,
        out_specs=P(("chan", "dm"), None, None, "bin"),
        check_vma=False,
    )
```

time: 71.5 us -> 58.4 us (0.82)
  blocking collectives: 38.2 us -> 18.8 us
  starting transfers between devices: 4.01 us -> 8.69 us
  Pallas kernels: 21.9 us -> 23.1 us
    all_to_all x2 -> x1, blocking collectives: 38.2 us -> 18.8 us  [shards(): lax.all_to_all(fold(own, far, up, down), ('chan', 'dm'), 0, 0, axis_index...]
    ppermute x2 -> x5, starting transfers between devices: 4.01 us -> 8.69 us  [the longest x3 6.59 us: moved(): lax.ppermute(x, 'chan', [(i, (i + s * cores) % chans) for i in range(chan...]
    pallas_call x4 -> x6, Pallas kernels: 21.9 us -> 23.1 us  [the longest x3 20.2 us: dedisperse(): pl.pallas_call(partial(channel_sums, period=period, offsets=offsets, hops...]
    ppermute x2 -> x5, waiting for transfers between devices: 4.14 us -> 4.66 us  [the longest x1 1.69 us: shards(): lax.ppermute(head, 'bin', [((i + 1) % bins, i) for i in range(bins)])]
    unnamed x5 -> x6, local copies, waits for them, and re-layouts: 2.01 us -> 2.36 us
  transfers between devices with their start and end apart: 2 -> 5, of which waited for: 1 -> 3; matrix products, arithmetic and copies ran while one was open for 0% -> 0% of each run, Pallas kernels for 0% -> 19%
where the time goes in v2:
time: 58.4 us; the launch traced here: 57.6 us
  Pallas kernels  23.1 us (40%)
  blocking collectives  18.8 us (32%)
  starting transfers between devices  8.69 us (15%)
  waiting for transfers between devices  4.66 us (8%)
  local copies, waits for them, and re-layouts  2.36 us (4%)
    pallas_call x3, Pallas kernels, dedisperse(): pl.pallas_call(partial(channel_sums, period=period, offsets=offsets, hops...  20.2 us
    all_to_all x1, blocking collectives, shards(): lax.all_to_all(fold(own, far, up, down), ('chan', 'dm'), 0, 0, axis_index...  18.8 us
    ppermute x3, starting transfers between devices, moved(): lax.ppermute(x, 'chan', [(i, (i + s * cores) % chans) for i in range(chan...  6.59 us
    pallas_call x1, Pallas kernels, response(): pl.pallas_call(response_kernel, grid_spec=pltpu.PrefetchScalarGridSpec(nu...  2.58 us
    unnamed x6, local copies, waits for them, and re-layouts  2.36 us
    ppermute x1, waiting for transfers between devices, shards(): lax.ppermute(head, 'bin', [((i + 1) % bins, i) for i in range(bins)])  1.69 us
    ppermute x1, starting transfers between devices, shards(): lax.ppermute(head, 'bin', [((i + 1) % bins, i) for i in range(bins)])  1.55 us
    ppermute x1, waiting for transfers between devices, shards(): left = lax.ppermute(tail, 'bin', [(i, (i + 1) % bins) for i in range(bins)])  1.54 us
  transfers between devices with their start and end apart: 5, of which 3 were waited for; matrix products, arithmetic and copies ran while one was open for 0% of the time, Pallas kernels for 19%

profile of v2, /device:TPU:6, one launch (start us, length us, event | category | flops | bytes accessed | tf_op | source)
XLA Modules:
  0.0 57.6 jit_solution(5010708847701094734)
XLA Ops:
  0.0 0.1 pad_add_fusion.place_ref
  0.1 0.0 copy-start
  0.1 1.6 %copy-done = bf16[2,4,128,1024]{3,2,1,0:T(8,128)(2,1)S(1)} copy-done((bf16[2,4,128,1024]{3,2,1,0:T(8,128)(2,1)S(1)}, bf16[2,4,128,1024]{3,2,1,0:T(8,128)(2,1)}, u32[]{:S(2)}) %copy-start) | copy-done | bytes 2097176
  1.7 0.0 copy-start.1
  1.7 0.8 %copy-done.1 = s32[128,64]{0,1:T(8,128)S(1)} copy-done((s32[128,64]{0,1:T(8,128)S(1)}, s32[128,64]{0,1:T(8,128)}, u32[]{:S(2)}) %copy-start.1) | copy-done | bytes 32792
  2.4 9.2 %channel_sums.3 = (bf16[2,512,128]{2,1,0:T(8,128)(2,1)S(1)}, bf16[64,256,128]{2,1,0:T(8,128)(2,1)S(1)}) custom-call(s32[3]{0:T(128)S(1)} %pad_add_fusion.place_ref, s32[64,128]{1,0:T(8,128)S(1)} %bitcast.4, bf16[2,4,128,1024]{3,2,1,0:T(8,128)(2,1)S(1)} %copy-done), custom_call_target="tpu_custom_call" | custom-call | tf_op jit(solution)/shard_map/channel_sums/pallas_call | solution.py:154
  11.6 3.3 %collective-permute-start = (bf16[2,512,128]{2,1,0:T(8,128)(2,1)S(1)}, bf16[2,512,128]{2,1,0:T(8,128)(2,1)S(1)}, u32[]{:S(2)}, u32[]{:S(2)}) collective-permute-start(bf16[2,512,128]{2,1,0:T(8,128)(2,1)S(1)} %get-tuple-element.13), channel_id=1, source_target_pairs={{0,128},{32,160},{64,192},{96,224},{128,0},{160,32},{192,64},{224,... | collective-permute-start | bytes 786440 | tf_op jit(solution)/shard_map/ppermute | solution.py:298
  14.9 6.7 %channel_sums.5 = (bf16[2,512,128]{2,1,0:T(8,128)(2,1)S(1)}, bf16[2,512,128]{2,1,0:T(8,128)(2,1)S(1)}) custom-call(s32[3]{0:T(128)S(1)} %pad_add_fusion.place_ref, s32[64,128]{1,0:T(8,128)S(1)} %bitcast.5, bf16[64,256,128]{2,1,0:T(8,128)(2,1)S(1)} %get-tuple-element.12.x_ref), custom_call_target="tpu_custom_call" | custom-call | tf_op jit(solution)/shard_map/channel_sums/pallas_call | solution.py:154
  21.6 0.0 copy-start.2
  21.6 0.8 %collective-permute-start.1 = (bf16[2,512,128]{2,1,0:T(8,128)(2,1)S(1)}, bf16[2,512,128]{2,1,0:T(8,128)(2,1)S(1)}, u32[]{:S(2)}, u32[]{:S(2)}) collective-permute-start(bf16[2,512,128]{2,1,0:T(8,128)(2,1)S(1)} %get-tuple-element.14), channel_id=1, source_target_pairs={{0,64},{32,96},{64,128},{96,160},{128,192},{160,224},{192,0},{224,... | collective-permute-start | bytes 786440 | tf_op jit(solution)/shard_map/ppermute | solution.py:298
  22.4 2.6 %collective-permute-start.2 = (bf16[2,512,128]{2,1,0:T(8,128)(2,1)S(1)}, bf16[2,512,128]{2,1,0:T(8,128)(2,1)S(1)}, u32[]{:S(2)}, u32[]{:S(2)}) collective-permute-start(bf16[2,512,128]{2,1,0:T(8,128)(2,1)S(1)} %get-tuple-element.15), channel_id=1, source_target_pairs={{0,192},{32,224},{64,0},{96,32},{128,64},{160,96},{192,128},{224,1... | collective-permute-start | bytes 786440 | tf_op jit(solution)/shard_map/ppermute | solution.py:298
  25.0 4.3 %channel_sums.4.own_ref = f32[2,512,128]{2,1,0:T(8,128)S(1)} custom-call(s32[3]{0:T(128)S(1)} %pad_add_fusion.place_ref, s32[64,128]{1,0:T(8,128)S(1)} %bitcast.6, bf16[64,256,128]{2,1,0:T(8,128)(2,1)S(1)} %get-tuple-element.12.x_ref), custom_call_target="tpu_custom_call" | custom-call | tf_op jit(solution)/shard_map/channel_sums/pallas_call | solution.py:154
  29.3 0.0 collective-permute-done.far_ref
  29.3 1.4 %collective-permute-done.1.up_ref = bf16[2,512,128]{2,1,0:T(8,128)(2,1)S(1)} collective-permute-done((bf16[2,512,128]{2,1,0:T(8,128)(2,1)S(1)}, bf16[2,512,128]{2,1,0:T(8,128)(2,1)S(1)}, u32[]{:S(2)}, u32[]{:S(2)}) %collective-permute-start.1) | collective-permute-done | bytes 262176 | tf_op jit(solution)/shard_map/ppermute | solution.py:298
  30.7 0.0 collective-permute-done.2.down_ref
  30.7 0.2 fold.1
  30.9 18.8 %all_to_all.5.x_ref = bf16[16,64,128]{2,1,0:T(8,128)(2,1)S(1)} all-to-all(bf16[16,64,128]{2,1,0:T(8,128)(2,1)S(1)} %fold.1), channel_id=1, replica_groups={{0,4,8,12,16,20,24,28,32,36,40,44,48,52,56,60},{64,68,72,76,80,84,88,92..., dimensions={0} | all-to-all | bytes 524288 | tf_op jit(solution)/shard_map/all_to_all | solution.py:310
  49.7 0.6 collective-permute-start.3
  50.3 1.5 %collective-permute-start.4 = (bf16[2,128]{1,0:T(2,128)(2,1)S(1)}, bf16[2,128]{1,0:T(2,128)(2,1)S(1)}, u32[]{:S(2)}, u32[]{:S(2)}) collective-permute-start(bf16[2,128]{1,0:T(2,128)(2,1)S(1)} %get-tuple-element.18), channel_id=1, source_target_pairs={{1,0},{2,1},{3,2},{0,3},{5,4},{6,5},{7,6},{4,7},{9,8},{10,9},{11,1... | collective-permute-start | bytes 1544 | tf_op jit(solution)/shard_map/ppermute | solution.py:316
  51.8 1.5 %collective-permute-done.3.left_ref = bf16[2,128]{1,0:T(2,128)(2,1)S(1)} collective-permute-done((bf16[2,128]{1,0:T(2,128)(2,1)S(1)}, bf16[2,128]{1,0:T(2,128)(2,1)S(1)}, u32[]{:S(2)}, u32[]{:S(2)}) %collective-permute-start.3) | collective-permute-done | bytes 544 | tf_op jit(solution)/shard_map/ppermute | solution.py:315
  53.4 1.7 %collective-permute-done.4.right_ref = bf16[2,128]{1,0:T(2,128)(2,1)S(1)} collective-permute-done((bf16[2,128]{1,0:T(2,128)(2,1)S(1)}, bf16[2,128]{1,0:T(2,128)(2,1)S(1)}, u32[]{:S(2)}, u32[]{:S(2)}) %collective-permute-start.4) | collective-permute-done | bytes 544 | tf_op jit(solution)/shard_map/ppermute | solution.py:316
  55.1 0.0 copy-done.2
  55.1 2.6 %response.1 = bf16[1,64,4,1024]{3,2,1,0:T(4,128)(2,1)} custom-call(s32[3]{0:T(128)S(1)} %pad_add_fusion.place_ref, bf16[64,128]{1,0:T(8,128)(2,1)S(1)} %get-tuple-element.16.y_ref, bf16[2,128]{1,0:T(2,128)(2,1)S(1)} %collective-permute-done.3.left_ref, bf16[2,128]{1,0:T(2,128)(2,1)S(1)} %collective-permute-done.4.right_ref, bf16[2,64,64]{2,1,0:T(8,128)(2,1)S(1)} %copy-done.2), custom_call_target="tpu_custom_call" | custom-call | tf_op jit(solution)/shard_map/response/pallas_call | solution.py:262
  (1 shorter events, 0.0 us)
Async XLA Ops:
  0.1 1.6 %copy-start = (bf16[2,4,128,1024]{3,2,1,0:T(8,128)(2,1)S(1)}, bf16[2,4,128,1024]{3,2,1,0:T(8,128)(2,1)}, u32[]{:S(2)}) copy-start(bf16[2,4,128,1024]{3,2,1,0:T(8,128)(2,1)} %x_ref.1) | copy-start | bytes 6291460
  1.7 0.8 %copy-start.1 = (s32[128,64]{0,1:T(8,128)S(1)}, s32[128,64]{0,1:T(8,128)}, u32[]{:S(2)}) copy-start(s32[128,64]{0,1:T(8,128)} %param.4) | copy-start | bytes 98308
  11.6 17.6 %collective-permute-start = (bf16[2,512,128]{2,1,0:T(8,128)(2,1)S(1)}, bf16[2,512,128]{2,1,0:T(8,128)(2,1)S(1)}, u32[]{:S(2)}, u32[]{:S(2)}) collective-permute-start(bf16[2,512,128]{2,1,0:T(8,128)(2,1)S(1)} %get-tuple-element.13), channel_id=1, source_target_pairs={{0,128},{32,160},{64,192},{96,224},{128,0},{160,32},{192,64},{224,... | collective-permute-start | bytes 786440 | tf_op jit(solution)/shard_map/ppermute | solution.py:298
  21.6 33.4 %copy-start.2 = (bf16[2,64,64]{2,1,0:T(8,128)(2,1)S(1)}, bf16[2,64,64]{2,1,0:T(8,128)(2,1)}, u32[]{:S(2)}) copy-start(bf16[2,64,64]{2,1,0:T(8,128)(2,1)} %h_ref.1) | copy-start | bytes 49156
  21.6 9.0 %collective-permute-start.1 = (bf16[2,512,128]{2,1,0:T(8,128)(2,1)S(1)}, bf16[2,512,128]{2,1,0:T(8,128)(2,1)S(1)}, u32[]{:S(2)}, u32[]{:S(2)}) collective-permute-start(bf16[2,512,128]{2,1,0:T(8,128)(2,1)S(1)} %get-tuple-element.14), channel_id=1, source_target_pairs={{0,64},{32,96},{64,128},{96,160},{128,192},{160,224},{192,0},{224,... | collective-permute-start | bytes 786440 | tf_op jit(solution)/shard_map/ppermute | solution.py:298
  22.4 8.3 %collective-permute-start.2 = (bf16[2,512,128]{2,1,0:T(8,128)(2,1)S(1)}, bf16[2,512,128]{2,1,0:T(8,128)(2,1)S(1)}, u32[]{:S(2)}, u32[]{:S(2)}) collective-permute-start(bf16[2,512,128]{2,1,0:T(8,128)(2,1)S(1)} %get-tuple-element.15), channel_id=1, source_target_pairs={{0,192},{32,224},{64,0},{96,32},{128,64},{160,96},{192,128},{224,1... | collective-permute-start | bytes 786440 | tf_op jit(solution)/shard_map/ppermute | solution.py:298
  49.7 3.6 %collective-permute-start.3 = (bf16[2,128]{1,0:T(2,128)(2,1)S(1)}, bf16[2,128]{1,0:T(2,128)(2,1)S(1)}, u32[]{:S(2)}, u32[]{:S(2)}) collective-permute-start(bf16[2,128]{1,0:T(2,128)(2,1)S(1)} %get-tuple-element.17), channel_id=1, source_target_pairs={{0,1},{1,2},{2,3},{3,0},{4,5},{5,6},{6,7},{7,4},{8,9},{9,10},{10,1... | collective-permute-start | bytes 1544 | tf_op jit(solution)/shard_map/ppermute | solution.py:315
  50.3 4.8 %collective-permute-start.4 = (bf16[2,128]{1,0:T(2,128)(2,1)S(1)}, bf16[2,128]{1,0:T(2,128)(2,1)S(1)}, u32[]{:S(2)}, u32[]{:S(2)}) collective-permute-start(bf16[2,128]{1,0:T(2,128)(2,1)S(1)} %get-tuple-element.18), channel_id=1, source_target_pairs={{1,0},{2,1},{3,2},{0,3},{5,4},{6,5},{7,6},{4,7},{9,8},{10,9},{11,1... | collective-permute-start | bytes 1544 | tf_op jit(solution)/shard_map/ppermute | solution.py:316

commit v3 on v2

v3 whole, which is shorter than its diff:
```python
import math
from functools import partial

import jax
import jax.numpy as jnp
from jax import lax
from jax.experimental import pallas as pl
from jax.experimental.pallas import tpu as pltpu
from jax.sharding import PartitionSpec as P

D = 64
BEAMS = 4
TEMPLATES = 64
TAPS = 64
GROUP = 16
TILE = 128
SUB = TILE // GROUP
LANES = 2 * BEAMS
PER_HOP = 16
STEPS = 2
PHASE_DT = jnp.bfloat16
F32 = jnp.float32
BF16 = jnp.bfloat16


def swap_blocks(tiles):
    tiles = list(tiles)
    lane = lax.broadcasted_iota(jnp.int32, tiles[0].shape, 1)
    for step in (4, 2, 1):
        upper = (lane // GROUP) & step != 0
        fresh = list(tiles)
        for low in range(SUB):
            if low & step == 0:
                high = low | step
                fresh[low] = jnp.where(upper, pltpu.roll(tiles[high], step * GROUP, 1), tiles[low])
                fresh[high] = jnp.where(
                    upper, tiles[high], pltpu.roll(tiles[low], TILE - step * GROUP, 1)
                )
        tiles = fresh
    return tiles


def unit(count, period):
    quarter = period // 4
    rest = (count & (period - 1)) + quarter // 2
    turns = rest // quarter
    x = ((rest & (quarter - 1)) - quarter // 2).astype(F32) * (2.0 * math.pi / period)
    z = x * x
    sine = x * (1.0 + z * (-1.0 / 6 + z * (1.0 / 120 + z * (-1.0 / 5040 + z * (1.0 / 362880)))))
    cosine = 1.0 + z * (-0.5 + z * (1.0 / 24 + z * (-1.0 / 720 + z * (1.0 / 40320))))
    odd = turns & 1 == 1
    first = jnp.where(odd, sine, cosine)
    second = jnp.where(odd, cosine, sine)
    return (
        jnp.where((turns + 1) & 2 == 2, -first, first),
        jnp.where(turns & 2 == 2, -second, second),
    )


def times(a, b):
    return a[0] * b[0] - a[1] * b[1], a[0] * b[1] + a[1] * b[0]


def near(x):
    return pltpu.with_memory_space_constraint(x, pltpu.VMEM)


def far_away(x):
    return pltpu.with_memory_space_constraint(x, pltpu.HBM)


def channel_sums(place_ref, delay_ref, x_ref, *rest, period, offsets, hops, build, per_step):
    outs = 2 if build else len(offsets)
    out_refs, rest = rest[:outs], rest[outs:]
    if build:
        w_ref, copy_ref, fine_ref, mid_ref, base_ref, native_ref, sems = rest

        def fetch(t):
            part = native_ref.shape[3] // STEPS
            span = pl.ds(pl.multiple_of(t * part, TILE), part)
            return pltpu.make_async_copy(x_ref.at[:, :, :, span], native_ref.at[:, :, :, span], sems.at[t])

    else:
        w_ref = x_ref
        fine_ref, mid_ref, base_ref = rest
    step = pl.program_id(0)
    half = GROUP // 2
    count = len(offsets) * PER_HOP

    @pl.when(step == 0)
    def _():
        if build:
            for t in range(STEPS):
                fetch(t).start()
            copy_ref[...] = delay_ref[...]
        n = jnp.concatenate(
            [
                delay_ref[pl.ds(pl.multiple_of((place_ref[1] + s) % hops * PER_HOP, PER_HOP), PER_HOP), :]
                for s in offsets
            ],
            axis=0,
        )
        one = unit(n, period)
        group = unit(n * GROUP, period)
        wide = unit(n * TILE, period)
        start = unit(n * place_ref[0], period)
        power = one
        for j in range(1, half + 1):
            fine_ref[0, j] = power[0].astype(PHASE_DT)
            fine_ref[1, j] = power[1].astype(PHASE_DT)
            if j == half:
                mid = power
            power = times(power, one)
        for g in range(SUB):
            mid_ref[0, g] = mid[0]
            mid_ref[1, g] = mid[1]
            mid = times(mid, group)
        base_ref[0] = start[0]
        base_ref[1] = start[1]
        base_ref[2] = wide[0]
        base_ref[3] = wide[1]

    if build:
        lanes = lax.broadcasted_iota(jnp.int32, (128, TILE), 1)
        fetch(step).wait()

    def build_weights(tile):
        span = pl.ds(pl.multiple_of(tile * TILE, TILE), TILE)
        native = [native_ref[j // BEAMS, j % BEAMS, :, span] for j in range(LANES)]
        for g, mixed in enumerate(swap_blocks(native)):
            at = tile * (SUB // 2) + g // 2
            side = pl.ds(g % 2 * TILE, TILE)
            w_ref[at, 0:128, side] = mixed
            turned = pltpu.roll(mixed, TILE // 2, 1)
            w_ref[at, 128:256, side] = jnp.where(lanes >= TILE // 2, -turned, turned)

    bin_of_lane = lax.broadcasted_iota(jnp.int32, (count, TILE), 1) & (GROUP - 1)

    def phases(base, g):
        turn = times(base, (mid_ref[0, g], mid_ref[1, g]))
        fc = turn[0].astype(PHASE_DT)
        fs = turn[1].astype(PHASE_DT)
        rows = [None] * GROUP
        rows[half] = (fc, fs)
        for j in range(1, half + 1):
            ec = fine_ref[0, j]
            es = fine_ref[1, j]
            cc = fc * ec
            ss = fs * es
            sc = fs * ec
            cs = fc * es
            if j < half:
                rows[half + j] = (cc - ss, sc + cs)
            rows[half - j] = (cc + ss, sc - cs)
        return [jnp.concatenate([c.astype(BF16), s.astype(BF16)], axis=1) for c, s in rows]

    def one_tile(tile, base):
        if build:
            build_weights(tile)
        for pair in range(SUB // 2):
            left = jnp.concatenate(phases(base, 2 * pair) + phases(base, 2 * pair + 1), axis=0)
            prod = jnp.dot(left, w_ref[tile * (SUB // 2) + pair], preferred_element_type=F32)
            sides = []
            for side in range(2):
                cols = slice(side * TILE, (side + 1) * TILE)
                first = side * GROUP * count
                acc = prod[first : first + count, cols]
                for k in range(1, GROUP):
                    row = first + k * count
                    acc = jnp.where(bin_of_lane == k, prod[row : row + count, cols], acc)
                sides.append(acc.reshape(count // 8, 8, TILE))
            both = jnp.concatenate(sides, axis=1)
            part = both.shape[0] // outs
            at = pl.ds(pl.multiple_of(tile * SUB * 8 + pair * 16, 16), 16)
            for i, out_ref in enumerate(out_refs):
                out_ref[:, at, :] = both[i * part : (i + 1) * part].astype(out_ref.dtype)

    base = (base_ref[0], base_ref[1])
    wide = (base_ref[2], base_ref[3])
    for sub in range(per_step):
        one_tile(step * per_step + sub, base)
        base = times(base, wide)
    base_ref[0] = base[0]
    base_ref[1] = base[1]


def dedisperse(x, delays, place, period, offsets, hops, build, dtype):
    tiles = x.shape[3] // TILE if build else x.shape[0] // (SUB // 2)
    count = len(offsets) * PER_HOP
    x_spec = pl.BlockSpec(memory_space=pl.ANY)
    stage = [pltpu.VMEM((2, BEAMS, 128, tiles * TILE), BF16), pltpu.SemaphoreType.DMA((STEPS,))]
    w_spec = pl.BlockSpec(memory_space=pltpu.VMEM)
    outs = 2 if build else len(offsets)
    part = count // 8 // outs
    out_specs = [pl.BlockSpec(memory_space=pltpu.VMEM)] * outs
    out_shapes = [pltpu.VMEM((part, tiles * SUB * 8, TILE), dtype)] * outs
    w_shape = pltpu.VMEM((tiles * SUB // 2, 256, 2 * TILE), BF16)
    return pl.pallas_call(
        partial(channel_sums, period=period, offsets=offsets, hops=hops, build=build, per_step=tiles // STEPS),
        grid_spec=pltpu.PrefetchScalarGridSpec(
            num_scalar_prefetch=1,
            grid=(STEPS,),
            in_specs=[
                pl.BlockSpec((D, 128), lambda i, s: (0, 0)) if build else w_spec,
                x_spec if build else w_spec,
            ],
            out_specs=out_specs + [w_spec, w_spec] * build,
            scratch_shapes=[
                pltpu.VMEM((2, GROUP // 2 + 1, count, 128), PHASE_DT),
                pltpu.VMEM((2, SUB, count, 128), F32),
                pltpu.VMEM((4, count, 128), F32),
            ]
            + stage * build,
        ),
        out_shape=out_shapes + [w_shape, pltpu.VMEM(delays.shape, delays.dtype)] * build,
        compiler_params=pltpu.CompilerParams(vmem_limit_bytes=24 * 2**20),
        name="channel_sums",
    )(place, far_away(delays) if build else near(delays), far_away(x) if build else near(x))


def fold_kernel(place_ref, own_ref, up_ref, down_ref, keep_ref, send_ref, sum_ref):
    core = place_ref[3]
    for which, out_ref in ((core, keep_ref), (1 - core, send_ref)):
        total = own_ref[which]
        for ref in (up_ref, down_ref):
            total = total + ref[which].astype(F32)
        sum_ref[...] = total
        for d in range(8):
            part = sum_ref[pl.ds(d, total.shape[0] // 8, stride=8), :]
            out_ref[d] = part.astype(out_ref.dtype)


def fold(place, own, up, down):
    _, rows, lanes = own.shape
    vmem = pl.BlockSpec(memory_space=pltpu.VMEM)
    return pl.pallas_call(
        fold_kernel,
        grid_spec=pltpu.PrefetchScalarGridSpec(
            num_scalar_prefetch=1,
            in_specs=[vmem] * 3,
            out_specs=[vmem] * 2,
            scratch_shapes=[pltpu.VMEM((rows, lanes), F32)],
        ),
        out_shape=[pltpu.VMEM((8, rows // 8, lanes), kind) for kind in (F32, BF16)],
        compiler_params=pltpu.CompilerParams(vmem_limit_bytes=24 * 2**20),
        name="fold",
    )(place, near(own), near(up), near(down))


def relay_kernel(up_ref, down_ref, first_ref, second_ref, up_out, down_out):
    for x_ref, far_ref, core, out_ref in ((up_ref, first_ref, 0, up_out), (down_ref, second_ref, 1, down_out)):
        out_ref[1 - core] = x_ref[1 - core].astype(BF16)
        out_ref[core] = (x_ref[core] + far_ref[0].astype(F32)).astype(BF16)


def relay(up, down, first, second):
    vmem = pl.BlockSpec(memory_space=pltpu.VMEM)
    return pl.pallas_call(
        relay_kernel,
        in_specs=[vmem] * 4,
        out_specs=[vmem] * 2,
        out_shape=[pltpu.VMEM(up.shape, BF16)] * 2,
        compiler_params=pltpu.CompilerParams(vmem_limit_bytes=24 * 2**20),
        name="relay",
    )(near(up), near(down), near(first), near(second))


def join_kernel(x_ref, y_ref, out_ref):
    out_ref[...] = (x_ref[...] + y_ref[...].astype(F32)).astype(BF16)


def join(kept, received):
    vmem = pl.BlockSpec(memory_space=pltpu.VMEM)
    return pl.pallas_call(
        join_kernel,
        in_specs=[vmem] * 2,
        out_specs=vmem,
        out_shape=pltpu.VMEM(kept.shape, BF16),
        compiler_params=pltpu.CompilerParams(vmem_limit_bytes=24 * 2**20),
        name="join",
    )(near(kept), near(received))


def finish_kernel(x_ref, out_ref, head_ref, tail_ref, *, scale):
    total = x_ref[0].astype(F32)
    for i in range(1, x_ref.shape[0]):
        total = total + x_ref[i].astype(F32)
    y = (total * scale).astype(BF16)
    edge = head_ref.shape[0]
    out_ref[...] = y
    head_ref[...] = y[:edge]
    tail_ref[...] = y[y.shape[0] - edge :]


def finish(received, scale, edge):
    rows, lanes = received.shape[1:]
    return pl.pallas_call(
        partial(finish_kernel, scale=scale),
        in_specs=[pl.BlockSpec(memory_space=pltpu.VMEM)] * 1,
        out_specs=[pl.BlockSpec(memory_space=pltpu.VMEM)] * 3,
        out_shape=[pltpu.VMEM((n, lanes), BF16) for n in (rows, edge, edge)],
        compiler_params=pltpu.CompilerParams(vmem_limit_bytes=24 * 2**20),
        name="finish",
    )(near(received))


def response_kernel(place_ref, y_ref, *rest, tiles, edges):
    if edges:
        left_ref, right_ref, h_ref, _, out_ref, u_ref, win_ref, pow_ref, part_ref, sems = rest
    else:
        h_ref, out_ref, u_ref, win_ref, pow_ref, part_ref, sems = rest
    rows = y_ref.shape[0]
    edge = TAPS // 2 // GROUP
    u_ref[...] = jnp.zeros(u_ref.shape, F32)
    u_ref[pl.ds(edge, rows), :] = y_ref[...].astype(F32)
    if edges:
        u_ref[0:edge, :] = jnp.where(place_ref[0] > 0, left_ref[...].astype(F32), 0.0)
        u_ref[pl.ds(edge + rows, edge), :] = jnp.where(place_ref[2] > 0, right_ref[...].astype(F32), 0.0)
    blocks = [u_ref[pl.ds(g, 16, stride=SUB), :] for g in range(SUB)]
    series = swap_blocks(blocks)
    for j in range(LANES):
        ri, beam = divmod(j, BEAMS)
        for i, m in enumerate(tiles):
            wide = jnp.concatenate([series[j][m : m + 1], series[j][m + 1 : m + 2]], axis=1)
            wide = jnp.broadcast_to(wide, (TAPS, 2 * TILE))
            turned = pltpu.roll(wide, 2 * TILE - (TAPS - 1), 1, stride=1, stride_axis=0)
            win_ref[beam, pl.ds(ri * TAPS, TAPS), pl.ds(i * TILE, TILE)] = turned[:, :TILE].astype(BF16)
    row = lax.broadcasted_iota(jnp.int32, (TAPS, TAPS), 0)
    col = lax.broadcasted_iota(jnp.int32, (TAPS, TAPS), 1)
    flip = jnp.where(row + col == TAPS - 1, 1.0, 0.0).astype(BF16)
    h_re = jnp.dot(h_ref[0], flip, preferred_element_type=F32)
    h_im = jnp.dot(h_ref[1], flip, preferred_element_type=F32)
    weights = jnp.concatenate(
        [jnp.concatenate([h_re, -h_im], axis=1), jnp.concatenate([h_im, h_re], axis=1)], axis=0
    ).astype(BF16)
    size = TEMPLATES * BEAMS
    for beam in range(BEAMS):
        resp = jnp.dot(weights, win_ref[beam], preferred_element_type=F32)
        re = resp[:TEMPLATES]
        im = resp[TEMPLATES:]
        power = re * re + im * im
        for i in range(len(tiles)):
            pow_ref[pl.ds(i * size + beam, TEMPLATES, stride=BEAMS), :] = power[:, i * TILE : (i + 1) * TILE]
    copies = []
    for i, m in enumerate(tiles):
        part = pow_ref[pl.ds(i * size, size), :]
        part_ref[i] = part.reshape(TEMPLATES, BEAMS, TILE).astype(BF16)
        copies.append(
            pltpu.make_async_copy(
                part_ref.at[i], out_ref.at[0, :, :, pl.ds(m * TILE, TILE)], sems.at[i]
            )
        )
        copies[-1].start()
    for copy in copies:
        copy.wait()


def response(place, y, templates, tiles, edges=(), before=()):
    width = y.shape[0] * GROUP
    count = len(tiles)
    vmem = pl.BlockSpec(memory_space=pltpu.VMEM)
    hbm = pl.BlockSpec(memory_space=pl.ANY)
    inputs = [near(y), *map(near, edges), templates]
    return pl.pallas_call(
        partial(response_kernel, tiles=tiles, edges=len(edges) > 0),
        grid_spec=pltpu.PrefetchScalarGridSpec(
            num_scalar_prefetch=1,
            in_specs=[vmem] * len(inputs) + [hbm] * len(before),
            out_specs=hbm,
            scratch_shapes=[
                pltpu.VMEM((16 * SUB, TILE), F32),
                pltpu.VMEM((BEAMS, 2 * TAPS, count * TILE), BF16),
                pltpu.VMEM((TEMPLATES * BEAMS * count, TILE), F32),
                pltpu.VMEM((count, TEMPLATES, BEAMS, TILE), BF16),
                pltpu.SemaphoreType.DMA((count,)),
            ],
        ),
        out_shape=jax.ShapeDtypeStruct((1, TEMPLATES, BEAMS, width), BF16),
        input_output_aliases={1 + len(inputs): 0} if before else {},
        compiler_params=pltpu.CompilerParams(vmem_limit_bytes=24 * 2**20),
        name="response",
    )(place, *inputs, *before)


def shards(spectra, delays, templates):
    width = spectra.shape[3]
    bins = lax.axis_size("bin")
    chans = lax.axis_size("chan")
    dms = lax.axis_size("dm")
    period = 2 * width * bins
    scale = 1.0 / math.sqrt(spectra.shape[2] * chans * dms)
    cores = PER_HOP // 8
    hops = chans // cores
    place = jnp.stack(
        [
            lax.axis_index("bin") * width,
            lax.axis_index("chan") // cores,
            bins - 1 - lax.axis_index("bin"),
            lax.axis_index("chan") % cores,
        ]
    ).astype(jnp.int32)
    table = delays.T

    def moved(x, s):
        return lax.ppermute(x, "chan", [(i, (i + s * cores) % chans) for i in range(chans)])

    first, second, weights, table = dedisperse(spectra, table, place, period, (2,), hops, True, BF16)
    first = moved(first, 1)
    second = moved(second, hops - 1)
    up, down = dedisperse(weights, table, place, period, (1, hops - 1), hops, False, F32)
    up, down = relay(up, down, first, second)
    up = moved(up, 1)
    down = moved(down, hops - 1)
    (own,) = dedisperse(weights, table, place, period, (0,), hops, False, F32)
    kept, sent = fold(place, own, up, down)
    other = lax.ppermute(
        sent, "chan", [(i, i // cores * cores + cores - 1 - i % cores) for i in range(chans)]
    )
    received = lax.all_to_all(join(kept, other), "dm", 0, 0, tiled=True)
    edge = TAPS // 2 // GROUP
    y, head, tail = finish(received, scale, edge)
    left = lax.ppermute(tail, "bin", [(i, (i + 1) % bins) for i in range(bins)])
    right = lax.ppermute(head, "bin", [((i + 1) % bins, i) for i in range(bins)])
    tiles = tuple(range(width // TILE))
    inner = response(place, y, templates, tiles[1:-1])
    return response(place, y, templates, (tiles[0], tiles[-1]), (left, right), (inner,))


def solution(mesh):
    placed = (P(None, None, ("chan", "dm"), "bin"), P(("chan", "dm"), None), P())
    return jax.shard_map(
        shards,
        mesh=mesh,
        in_specs=placed,
        out_specs=P(("chan", "dm"), None, None, "bin"),
        check_vma=False,
    )
```

time: 58.4 us -> 53.5 us (0.916)
  local copies, waits for them, and re-layouts: 2.36 us -> 0.01 us
  Pallas kernels: 23.1 us -> 21.7 us
  blocking collectives: 18.8 us -> 17.6 us
    pallas_call x3, Pallas kernels: 20.2 us -> 16.7 us  [dedisperse(): pl.pallas_call(partial(channel_sums, period=period, offsets=offsets, hops...]
    unnamed x6 -> x2, local copies, waits for them, and re-layouts: 2.36 us -> 0.01 us
    pallas_call x2 -> x5, Pallas kernels: 2.8 us -> 4.99 us  [the longest x2 4.17 us: response(): pl.pallas_call(partial(response_kernel, tiles=tiles, edges=len(edges) > 0...]
    ppermute x1, waiting for transfers between devices: 1.54 us -> 0.01 us  [shards(): left = lax.ppermute(tail, 'bin', [(i, (i + 1) % bins) for i in range(bins)])]
    ppermute x0 -> x1, waiting for transfers between devices: none -> 1.33 us  [shards(): lax.ppermute(sent, 'chan', [(i, i // cores * cores + cores - 1 - i % core...]
    all_to_all x1, blocking collectives: 18.8 us -> 17.6 us  [shards(): received = lax.all_to_all(join(kept, other), 'dm', 0, 0, tiled=True)]
    ppermute x3 -> x4, waiting for transfers between devices: 1.43 us -> 2.39 us  [moved(): lax.ppermute(x, 'chan', [(i, (i + s * cores) % chans) for i in range(chan...]
    ppermute x1, waiting for transfers between devices: 1.69 us -> 0.9 us  [shards(): lax.ppermute(head, 'bin', [((i + 1) % bins, i) for i in range(bins)])]
  transfers between devices with their start and end apart: 5 -> 7, of which waited for: 3 -> 3; matrix products, arithmetic and copies ran while one was open for 0% -> 0% of each run, Pallas kernels for 19% -> 21%
where the time goes in v3:
time: 53.5 us; the launch traced here: 53 us
  Pallas kernels  21.7 us (41%)
  blocking collectives  17.6 us (33%)
  starting transfers between devices  8.82 us (16%)
  waiting for transfers between devices  4.63 us (9%)
    all_to_all x1, blocking collectives, shards(): received = lax.all_to_all(join(kept, other), 'dm', 0, 0, tiled=True)  17.6 us
    pallas_call x3, Pallas kernels, dedisperse(): pl.pallas_call(partial(channel_sums, period=period, offsets=offsets, hops...  16.7 us
    ppermute x4, starting transfers between devices, moved(): lax.ppermute(x, 'chan', [(i, (i + s * cores) % chans) for i in range(chan...  6.63 us
    pallas_call x2, Pallas kernels, response(): pl.pallas_call(partial(response_kernel, tiles=tiles, edges=len(edges) > 0...  4.17 us
    ppermute x4, waiting for transfers between devices, moved(): lax.ppermute(x, 'chan', [(i, (i + s * cores) % chans) for i in range(chan...  2.39 us
    ppermute x1, starting transfers between devices, shards(): lax.ppermute(head, 'bin', [((i + 1) % bins, i) for i in range(bins)])  1.54 us
    ppermute x1, waiting for transfers between devices, shards(): lax.ppermute(sent, 'chan', [(i, i // cores * cores + cores - 1 - i % core...  1.33 us
  transfers between devices with their start and end apart: 7, of which 3 were waited for; matrix products, arithmetic and copies ran while one was open for 0% of the time, Pallas kernels for 21%

profile of v3, /device:TPU:6, one launch (start us, length us, event | category | flops | bytes accessed | tf_op | source)
XLA Modules:
  0.0 53.0 jit_solution(15106515952502502882)
XLA Ops:
  0.0 0.1 pad_add_fusion.place_ref
  0.1 8.0 %channel_sums.3 = (bf16[1,512,128]{2,1,0:T(8,128)(2,1)S(1)}, bf16[1,512,128]{2,1,0:T(8,128)(2,1)S(1)}, bf16[32,256,256]{2,1,0:T(8,128)(2,1)S(1)}, s32[64,128]{1,0:T(8,128)S(1)}) custom-call(s32[4]{0:T(128)S(1)} %pad_add_fusion.place_ref, s32[64,128]{1,0:T(8,128)} %bitcast.5, bf16[2,4,128,1024]{3,2,1,0:T(8,128)(2,1)} %x_ref.1), custom_call_target="tpu_custom_call" | custom-call | tf_op jit(solution)/shard_map/channel_sums/pallas_call | solution.py:198
  8.1 1.7 %collective-permute-start = (bf16[1,512,128]{2,1,0:T(8,128)(2,1)S(1)}, bf16[1,512,128]{2,1,0:T(8,128)(2,1)S(1)}, u32[]{:S(2)}, u32[]{:S(2)}) collective-permute-start(bf16[1,512,128]{2,1,0:T(8,128)(2,1)S(1)} %get-tuple-element.22), channel_id=1, source_target_pairs={{0,64},{32,96},{64,128},{96,160},{128,192},{160,224},{192,0},{224,... | collective-permute-start | bytes 393224 | tf_op jit(solution)/shard_map/ppermute | solution.py:405
  9.8 1.7 %collective-permute-start.1 = (bf16[1,512,128]{2,1,0:T(8,128)(2,1)S(1)}, bf16[1,512,128]{2,1,0:T(8,128)(2,1)S(1)}, u32[]{:S(2)}, u32[]{:S(2)}) collective-permute-start(bf16[1,512,128]{2,1,0:T(8,128)(2,1)S(1)} %get-tuple-element.23), channel_id=1, source_target_pairs={{0,192},{32,224},{64,0},{96,32},{128,64},{160,96},{192,128},{224,1... | collective-permute-start | bytes 393224 | tf_op jit(solution)/shard_map/ppermute | solution.py:405
  11.4 5.5 %channel_sums.5 = (f32[2,512,128]{2,1,0:T(8,128)S(1)}, f32[2,512,128]{2,1,0:T(8,128)S(1)}) custom-call(s32[4]{0:T(128)S(1)} %pad_add_fusion.place_ref, s32[64,128]{1,0:T(8,128)S(1)} %get-tuple-element.18.delay_ref, bf16[32,256,256]{2,1,0:T(8,128)(2,1)S(1)} %get-tuple-element.19.x_ref), custom_call_target="tpu_custom_call" | custom-call | tf_op jit(solution)/shard_map/channel_sums/pallas_call | solution.py:198
  16.9 0.0 copy-start
  16.9 0.0 collective-permute-done.first_ref
  16.9 0.0 collective-permute-done.1.second_ref
  16.9 0.1 relay.1
  17.0 0.4 collective-permute-start.2
  17.5 2.9 %collective-permute-start.3 = (bf16[2,512,128]{2,1,0:T(8,128)(2,1)S(1)}, bf16[2,512,128]{2,1,0:T(8,128)(2,1)S(1)}, u32[]{:S(2)}, u32[]{:S(2)}) collective-permute-start(bf16[2,512,128]{2,1,0:T(8,128)(2,1)S(1)} %get-tuple-element.25), channel_id=1, source_target_pairs={{0,192},{32,224},{64,0},{96,32},{128,64},{160,96},{192,128},{224,1... | collective-permute-start | bytes 786440 | tf_op jit(solution)/shard_map/ppermute | solution.py:405
  20.3 3.2 %channel_sums.4.own_ref = f32[2,512,128]{2,1,0:T(8,128)S(1)} custom-call(s32[4]{0:T(128)S(1)} %pad_add_fusion.place_ref, s32[64,128]{1,0:T(8,128)S(1)} %get-tuple-element.18.delay_ref, bf16[32,256,256]{2,1,0:T(8,128)(2,1)S(1)} %get-tuple-element.19.x_ref), custom_call_target="tpu_custom_call" | custom-call | tf_op jit(solution)/shard_map/channel_sums/pallas_call | solution.py:198
  23.6 2.4 %collective-permute-done.2.up_ref = bf16[2,512,128]{2,1,0:T(8,128)(2,1)S(1)} collective-permute-done((bf16[2,512,128]{2,1,0:T(8,128)(2,1)S(1)}, bf16[2,512,128]{2,1,0:T(8,128)(2,1)S(1)}, u32[]{:S(2)}, u32[]{:S(2)}) %collective-permute-start.2) | collective-permute-done | bytes 262176 | tf_op jit(solution)/shard_map/ppermute | solution.py:405
  26.0 0.0 collective-permute-done.3.down_ref
  26.0 0.7 %fold.1 = (f32[8,64,128]{2,1,0:T(8,128)S(1)}, bf16[8,64,128]{2,1,0:T(8,128)(2,1)S(1)}) custom-call(s32[4]{0:T(128)S(1)} %pad_add_fusion.place_ref, f32[2,512,128]{2,1,0:T(8,128)S(1)} %channel_sums.4.own_ref, bf16[2,512,128]{2,1,0:T(8,128)(2,1)S(1)} %collective-permute-done.2.up_ref, bf16[2,512,128]{2,1,0:T(8,128)(2,1)S(1)} %collective-permute-done.3.down_ref), custom_call_target="tpu_custom_call" | custom-call | tf_op jit(solution)/shard_map/fold/pallas_call | solution.py:236
  26.7 0.1 collective-permute-start.4
  26.8 1.3 %collective-permute-done.4.y_ref = bf16[8,64,128]{2,1,0:T(8,128)(2,1)S(1)} collective-permute-done((bf16[8,64,128]{2,1,0:T(8,128)(2,1)S(1)}, bf16[8,64,128]{2,1,0:T(8,128)(2,1)S(1)}, u32[]{:S(2)}, u32[]{:S(2)}) %collective-permute-start.4) | collective-permute-done | bytes 131104 | tf_op jit(solution)/shard_map/ppermute | solution.py:416
  28.1 17.6 %all_to_all.5.x_ref = bf16[8,64,128]{2,1,0:T(8,128)(2,1)S(1)} all-to-all(bf16[8,64,128]{2,1,0:T(8,128)(2,1)S(1)} %join.1), channel_id=1, replica_groups=mesh['chan'=8,'dm'=8,'bin'=4] {'dm'}, dimensions={0} | all-to-all | bytes 262144 | tf_op jit(solution)/shard_map/all_to_all | solution.py:419
  45.8 0.6 %collective-permute-start.5 = (bf16[2,128]{1,0:T(2,128)(2,1)S(1)}, bf16[2,128]{1,0:T(2,128)(2,1)S(1)}, u32[]{:S(2)}, u32[]{:S(2)}) collective-permute-start(bf16[2,128]{1,0:T(2,128)(2,1)S(1)} %get-tuple-element.29), channel_id=1, source_target_pairs={{0,1},{1,2},{2,3},{3,0},{4,5},{5,6},{6,7},{7,4},{8,9},{9,10},{10,1... | collective-permute-start | bytes 1544 | tf_op jit(solution)/shard_map/ppermute | solution.py:422
  46.4 1.5 %collective-permute-start.6 = (bf16[2,128]{1,0:T(2,128)(2,1)S(1)}, bf16[2,128]{1,0:T(2,128)(2,1)S(1)}, u32[]{:S(2)}, u32[]{:S(2)}) collective-permute-start(bf16[2,128]{1,0:T(2,128)(2,1)S(1)} %get-tuple-element.30), channel_id=1, source_target_pairs={{1,0},{2,1},{3,2},{0,3},{5,4},{6,5},{7,6},{4,7},{9,8},{10,9},{11,1... | collective-permute-start | bytes 1544 | tf_op jit(solution)/shard_map/ppermute | solution.py:423
  47.9 0.0 copy-done
  47.9 2.3 %response.2.rest_3_ = bf16[1,64,4,1024]{3,2,1,0:T(4,128)(2,1)} custom-call(s32[4]{0:T(128)S(1)} %pad_add_fusion.place_ref, bf16[64,128]{1,0:T(8,128)(2,1)S(1)} %get-tuple-element.28.y_ref, bf16[2,64,64]{2,1,0:T(8,128)(2,1)S(1)} %copy-done), custom_call_target="tpu_custom_call" | custom-call | tf_op jit(solution)/shard_map/response/pallas_call | solution.py:364
  50.2 0.0 collective-permute-done.5.rest_0_
  50.2 0.9 %collective-permute-done.6.rest_1_ = bf16[2,128]{1,0:T(2,128)(2,1)S(1)} collective-permute-done((bf16[2,128]{1,0:T(2,128)(2,1)S(1)}, bf16[2,128]{1,0:T(2,128)(2,1)S(1)}, u32[]{:S(2)}, u32[]{:S(2)}) %collective-permute-start.6) | collective-permute-done | bytes 544 | tf_op jit(solution)/shard_map/ppermute | solution.py:423
  51.2 1.9 %response.3 = bf16[1,64,4,1024]{3,2,1,0:T(4,128)(2,1)} custom-call(s32[4]{0:T(128)S(1)} %pad_add_fusion.place_ref, bf16[64,128]{1,0:T(8,128)(2,1)S(1)} %get-tuple-element.28.y_ref, bf16[2,128]{1,0:T(2,128)(2,1)S(1)} %collective-permute-done.5.rest_0_, bf16[2,128]{1,0:T(2,128)(2,1)S(1)} %collective-permute-done.6.rest_1_, ...), custom_call_target="tpu_custom_call", output_to_operand_aliasing={{}: (5, {})} | custom-call | tf_op jit(solution)/shard_map/response/pallas_call | solution.py:364
  (2 shorter events, 0.1 us)
Async XLA Ops:
  8.1 8.8 %collective-permute-start = (bf16[1,512,128]{2,1,0:T(8,128)(2,1)S(1)}, bf16[1,512,128]{2,1,0:T(8,128)(2,1)S(1)}, u32[]{:S(2)}, u32[]{:S(2)}) collective-permute-start(bf16[1,512,128]{2,1,0:T(8,128)(2,1)S(1)} %get-tuple-element.22), channel_id=1, source_target_pairs={{0,64},{32,96},{64,128},{96,160},{128,192},{160,224},{192,0},{224,... | collective-permute-start | bytes 393224 | tf_op jit(solution)/shard_map/ppermute | solution.py:405
  9.8 7.2 %collective-permute-start.1 = (bf16[1,512,128]{2,1,0:T(8,128)(2,1)S(1)}, bf16[1,512,128]{2,1,0:T(8,128)(2,1)S(1)}, u32[]{:S(2)}, u32[]{:S(2)}) collective-permute-start(bf16[1,512,128]{2,1,0:T(8,128)(2,1)S(1)} %get-tuple-element.23), channel_id=1, source_target_pairs={{0,192},{32,224},{64,0},{96,32},{128,64},{160,96},{192,128},{224,1... | collective-permute-start | bytes 393224 | tf_op jit(solution)/shard_map/ppermute | solution.py:405
  16.9 31.0 %copy-start = (bf16[2,64,64]{2,1,0:T(8,128)(2,1)S(1)}, bf16[2,64,64]{2,1,0:T(8,128)(2,1)}, u32[]{:S(2)}) copy-start(bf16[2,64,64]{2,1,0:T(8,128)(2,1)} %rest_2_.1) | copy-start | bytes 49156
  17.0 8.9 %collective-permute-start.2 = (bf16[2,512,128]{2,1,0:T(8,128)(2,1)S(1)}, bf16[2,512,128]{2,1,0:T(8,128)(2,1)S(1)}, u32[]{:S(2)}, u32[]{:S(2)}) collective-permute-start(bf16[2,512,128]{2,1,0:T(8,128)(2,1)S(1)} %get-tuple-element.24), channel_id=1, source_target_pairs={{0,64},{32,96},{64,128},{96,160},{128,192},{160,224},{192,0},{224,... | collective-permute-start | bytes 786440 | tf_op jit(solution)/shard_map/ppermute | solution.py:405
  17.5 8.5 %collective-permute-start.3 = (bf16[2,512,128]{2,1,0:T(8,128)(2,1)S(1)}, bf16[2,512,128]{2,1,0:T(8,128)(2,1)S(1)}, u32[]{:S(2)}, u32[]{:S(2)}) collective-permute-start(bf16[2,512,128]{2,1,0:T(8,128)(2,1)S(1)} %get-tuple-element.25), channel_id=1, source_target_pairs={{0,192},{32,224},{64,0},{96,32},{128,64},{160,96},{192,128},{224,1... | collective-permute-start | bytes 786440 | tf_op jit(solution)/shard_map/ppermute | solution.py:405
  26.7 1.4 %collective-permute-start.4 = (bf16[8,64,128]{2,1,0:T(8,128)(2,1)S(1)}, bf16[8,64,128]{2,1,0:T(8,128)(2,1)S(1)}, u32[]{:S(2)}, u32[]{:S(2)}) collective-permute-start(bf16[8,64,128]{2,1,0:T(8,128)(2,1)S(1)} %get-tuple-element.27), channel_id=1, source_target_pairs={{0,32},{32,0},{64,96},{96,64},{128,160},{160,128},{192,224},{224,1... | collective-permute-start | bytes 393224 | tf_op jit(solution)/shard_map/ppermute | solution.py:416
  45.8 4.4 %collective-permute-start.5 = (bf16[2,128]{1,0:T(2,128)(2,1)S(1)}, bf16[2,128]{1,0:T(2,128)(2,1)S(1)}, u32[]{:S(2)}, u32[]{:S(2)}) collective-permute-start(bf16[2,128]{1,0:T(2,128)(2,1)S(1)} %get-tuple-element.29), channel_id=1, source_target_pairs={{0,1},{1,2},{2,3},{3,0},{4,5},{5,6},{6,7},{7,4},{8,9},{9,10},{10,1... | collective-permute-start | bytes 1544 | tf_op jit(solution)/shard_map/ppermute | solution.py:422
  46.4 4.8 %collective-permute-start.6 = (bf16[2,128]{1,0:T(2,128)(2,1)S(1)}, bf16[2,128]{1,0:T(2,128)(2,1)S(1)}, u32[]{:S(2)}, u32[]{:S(2)}) collective-permute-start(bf16[2,128]{1,0:T(2,128)(2,1)S(1)} %get-tuple-element.30), channel_id=1, source_target_pairs={{1,0},{2,1},{3,2},{0,3},{5,4},{6,5},{7,6},{4,7},{9,8},{10,9},{11,1... | collective-permute-start | bytes 1544 | tf_op jit(solution)/shard_map/ppermute | solution.py:423

commit v4 on v3

--- a/solution.py
+++ b/solution.py
@@ -18,6 +18,7 @@
 LANES = 2 * BEAMS
 PER_HOP = 16
 STEPS = 2
+PIECES = 4
 PHASE_DT = jnp.bfloat16
 F32 = jnp.float32
 BF16 = jnp.bfloat16
@@ -69,14 +70,14 @@
     return pltpu.with_memory_space_constraint(x, pltpu.HBM)
 
 
-def channel_sums(place_ref, delay_ref, x_ref, *rest, period, offsets, hops, build, per_step):
-    outs = 2 if build else len(offsets)
+def channel_sums(place_ref, delay_ref, x_ref, *rest, period, hops, build, per_step):
+    outs = 1
     out_refs, rest = rest[:outs], rest[outs:]
     if build:
         w_ref, copy_ref, fine_ref, mid_ref, base_ref, native_ref, sems = rest
 
         def fetch(t):
-            part = native_ref.shape[3] // STEPS
+            part = native_ref.shape[3] // PIECES
             span = pl.ds(pl.multiple_of(t * part, TILE), part)
             return pltpu.make_async_copy(x_ref.at[:, :, :, span], native_ref.at[:, :, :, span], sems.at[t])
 
@@ -85,21 +86,17 @@
         fine_ref, mid_ref, base_ref = rest
     step = pl.program_id(0)
     half = GROUP // 2
-    count = len(offsets) * PER_HOP
+    count = hops * 8
 
     @pl.when(step == 0)
     def _():
         if build:
-            for t in range(STEPS):
+            for t in range(PIECES):
                 fetch(t).start()
             copy_ref[...] = delay_ref[...]
-        n = jnp.concatenate(
-            [
-                delay_ref[pl.ds(pl.multiple_of((place_ref[1] + s) % hops * PER_HOP, PER_HOP), PER_HOP), :]
-                for s in offsets
-            ],
-            axis=0,
-        )
+        core = 1 - place_ref[3] if build else place_ref[3]
+        first_rows = [(place_ref[1] + s) % hops * PER_HOP + core * 8 for s in range(hops)]
+        n = jnp.concatenate([delay_ref[pl.ds(pl.multiple_of(r, 8), 8), :] for r in first_rows], axis=0)
         one = unit(n, period)
         group = unit(n * GROUP, period)
         wide = unit(n * TILE, period)
@@ -122,17 +119,15 @@
 
     if build:
         lanes = lax.broadcasted_iota(jnp.int32, (128, TILE), 1)
-        fetch(step).wait()
 
     def build_weights(tile):
         span = pl.ds(pl.multiple_of(tile * TILE, TILE), TILE)
         native = [native_ref[j // BEAMS, j % BEAMS, :, span] for j in range(LANES)]
         for g, mixed in enumerate(swap_blocks(native)):
             at = tile * (SUB // 2) + g // 2
-            side = pl.ds(g % 2 * TILE, TILE)
-            w_ref[at, 0:128, side] = mixed
+            w_ref[at, g % 2, 0:128] = mixed
             turned = pltpu.roll(mixed, TILE // 2, 1)
-            w_ref[at, 128:256, side] = jnp.where(lanes >= TILE // 2, -turned, turned)
+            w_ref[at, g % 2, 128:256] = jnp.where(lanes >= TILE // 2, -turned, turned)
 
     bin_of_lane = lax.broadcasted_iota(jnp.int32, (count, TILE), 1) & (GROUP - 1)
 
@@ -159,7 +154,9 @@
             build_weights(tile)
         for pair in range(SUB // 2):
             left = jnp.concatenate(phases(base, 2 * pair) + phases(base, 2 * pair + 1), axis=0)
-            prod = jnp.dot(left, w_ref[tile * (SUB // 2) + pair], preferred_element_type=F32)
+            at = tile * (SUB // 2) + pair
+            right = jnp.concatenate([w_ref[at, 0], w_ref[at, 1]], axis=1)
+            prod = jnp.dot(left, right, preferred_element_type=F32)
             sides = []
             for side in range(2):
                 cols = slice(side * TILE, (side + 1) * TILE)
@@ -177,26 +174,29 @@
 
     base = (base_ref[0], base_ref[1])
     wide = (base_ref[2], base_ref[3])
+    per_piece = per_step * STEPS // PIECES
     for sub in range(per_step):
+        if build and sub % per_piece == 0:
+            fetch(step * (PIECES // STEPS) + sub // per_piece).wait()
         one_tile(step * per_step + sub, base)
         base = times(base, wide)
     base_ref[0] = base[0]
     base_ref[1] = base[1]
 
 
-def dedisperse(x, delays, place, period, offsets, hops, build, dtype):
+def dedisperse(x, delays, place, period, hops, build, dtype):
     tiles = x.shape[3] // TILE if build else x.shape[0] // (SUB // 2)
-    count = len(offsets) * PER_HOP
+    count = hops * 8
     x_spec = pl.BlockSpec(memory_space=pl.ANY)
-    stage = [pltpu.VMEM((2, BEAMS, 128, tiles * TILE), BF16), pltpu.SemaphoreType.DMA((STEPS,))]
+    stage = [pltpu.VMEM((2, BEAMS, 128, tiles * TILE), BF16), pltpu.SemaphoreType.DMA((PIECES,))]
     w_spec = pl.BlockSpec(memory_space=pltpu.VMEM)
-    outs = 2 if build else len(offsets)
+    outs = 1
     part = count // 8 // outs
     out_specs = [pl.BlockSpec(memory_space=pltpu.VMEM)] * outs
     out_shapes = [pltpu.VMEM((part, tiles * SUB * 8, TILE), dtype)] * outs
-    w_shape = pltpu.VMEM((tiles * SUB // 2, 256, 2 * TILE), BF16)
+    w_shape = pltpu.VMEM((tiles * SUB // 2, 2, 256, TILE), BF16)
     return pl.pallas_call(
-        partial(channel_sums, period=period, offsets=offsets, hops=hops, build=build, per_step=tiles // STEPS),
+        partial(channel_sums, period=period, hops=hops, build=build, per_step=tiles // STEPS),
         grid_spec=pltpu.PrefetchScalarGridSpec(
             num_scalar_prefetch=1,
             grid=(STEPS,),
@@ -218,67 +218,47 @@
     )(place, far_away(delays) if build else near(delays), far_away(x) if build else near(x))
 
 
-def fold_kernel(place_ref, own_ref, up_ref, down_ref, keep_ref, send_ref, sum_ref):
-    core = place_ref[3]
-    for which, out_ref in ((core, keep_ref), (1 - core, send_ref)):
-        total = own_ref[which]
-        for ref in (up_ref, down_ref):
-            total = total + ref[which].astype(F32)
-        sum_ref[...] = total
-        for d in range(8):
-            part = sum_ref[pl.ds(d, total.shape[0] // 8, stride=8), :]
-            out_ref[d] = part.astype(out_ref.dtype)
-
-
-def fold(place, own, up, down):
-    _, rows, lanes = own.shape
+def join_kernel(mine_ref, other_ref, keep_ref, *send_refs):
+    keep_ref[...] = mine_ref[0] + other_ref[0].astype(F32)
+    for s, send_ref in enumerate(send_refs, 1):
+        send_ref[...] = (mine_ref[s] + other_ref[s].astype(F32)).astype(BF16)
+
+
+def join(mine, other):
+    vmem = pl.BlockSpec(memory_space=pltpu.VMEM)
+    hops, rows, lanes = mine.shape
+    return pl.pallas_call(
+        join_kernel,
+        in_specs=[vmem] * 2,
+        out_specs=[vmem] * hops,
+        out_shape=[pltpu.VMEM((rows, lanes), kind) for kind in [F32] + [BF16] * (hops - 1)],
+        compiler_params=pltpu.CompilerParams(vmem_limit_bytes=24 * 2**20),
+        name="join",
+    )(near(mine), near(other))
+
+
+def fold_kernel(keep_ref, *rest):
+    *got_refs, out_ref, sum_ref = rest
+    total = keep_ref[...]
+    for ref in got_refs:
+        total = total + ref[...].astype(F32)
+    sum_ref[...] = total
+    for d in range(8):
+        out_ref[d] = sum_ref[pl.ds(d, total.shape[0] // 8, stride=8), :].astype(BF16)
+
+
+def fold(kept, received):
+    rows, lanes = kept.shape
     vmem = pl.BlockSpec(memory_space=pltpu.VMEM)
     return pl.pallas_call(
         fold_kernel,
-        grid_spec=pltpu.PrefetchScalarGridSpec(
-            num_scalar_prefetch=1,
-            in_specs=[vmem] * 3,
-            out_specs=[vmem] * 2,
-            scratch_shapes=[pltpu.VMEM((rows, lanes), F32)],
-        ),
-        out_shape=[pltpu.VMEM((8, rows // 8, lanes), kind) for kind in (F32, BF16)],
+        in_specs=[vmem] * (1 + len(received)),
+        out_specs=vmem,
+        out_shape=pltpu.VMEM((8, rows // 8, lanes), BF16),
+        scratch_shapes=[pltpu.VMEM((rows, lanes), F32)],
         compiler_params=pltpu.CompilerParams(vmem_limit_bytes=24 * 2**20),
         name="fold",
-    )(place, near(own), near(up), near(down))
-
-
-def relay_kernel(up_ref, down_ref, first_ref, second_ref, up_out, down_out):
-    for x_ref, far_ref, core, out_ref in ((up_ref, first_ref, 0, up_out), (down_ref, second_ref, 1, down_out)):
-        out_ref[1 - core] = x_ref[1 - core].astype(BF16)
-        out_ref[core] = (x_ref[core] + far_ref[0].astype(F32)).astype(BF16)
-
-
-def relay(up, down, first, second):
-    vmem = pl.BlockSpec(memory_space=pltpu.VMEM)
-    return pl.pallas_call(
-        relay_kernel,
-        in_specs=[vmem] * 4,
-        out_specs=[vmem] * 2,
-        out_shape=[pltpu.VMEM(up.shape, BF16)] * 2,
-        compiler_params=pltpu.CompilerParams(vmem_limit_bytes=24 * 2**20),
-        name="relay",
-    )(near(up), near(down), near(first), near(second))
-
-
-def join_kernel(x_ref, y_ref, out_ref):
-    out_ref[...] = (x_ref[...] + y_ref[...].astype(F32)).astype(BF16)
-
-
-def join(kept, received):
-    vmem = pl.BlockSpec(memory_space=pltpu.VMEM)
-    return pl.pallas_call(
-        join_kernel,
-        in_specs=[vmem] * 2,
-        out_specs=vmem,
-        out_shape=pltpu.VMEM(kept.shape, BF16),
-        compiler_params=pltpu.CompilerParams(vmem_limit_bytes=24 * 2**20),
-        name="join",
-    )(near(kept), near(received))
+    )(near(kept), *map(near, received))
 
 
 def finish_kernel(x_ref, out_ref, head_ref, tail_ref, *, scale):
@@ -404,19 +384,15 @@
     def moved(x, s):
         return lax.ppermute(x, "chan", [(i, (i + s * cores) % chans) for i in range(chans)])
 
-    first, second, weights, table = dedisperse(spectra, table, place, period, (2,), hops, True, BF16)
-    first = moved(first, 1)
-    second = moved(second, hops - 1)
-    up, down = dedisperse(weights, table, place, period, (1, hops - 1), hops, False, F32)
-    up, down = relay(up, down, first, second)
-    up = moved(up, 1)
-    down = moved(down, hops - 1)
-    (own,) = dedisperse(weights, table, place, period, (0,), hops, False, F32)
-    kept, sent = fold(place, own, up, down)
+    other, weights, table = dedisperse(spectra, table, place, period, hops, True, BF16)
     other = lax.ppermute(
-        sent, "chan", [(i, i // cores * cores + cores - 1 - i % cores) for i in range(chans)]
+        other, "chan", [(i, i // cores * cores + cores - 1 - i % cores) for i in range(chans)]
     )
-    received = lax.all_to_all(join(kept, other), "dm", 0, 0, tiled=True)
+    (mine,) = dedisperse(weights, table, place, period, hops, False, F32)
+    kept, *sent = join(mine, other)
+    order = sorted(range(1, hops), key=lambda s: -min(s, hops - s))
+    received = [moved(sent[s - 1], s) for s in order]
+    received = lax.all_to_all(fold(kept, received), "dm", 0, 0, tiled=True)
     edge = TAPS // 2 // GROUP
     y, head, tail = finish(received, scale, edge)
     left = lax.ppermute(tail, "bin", [(i, (i + 1) % bins) for i in range(bins)])

time: 53.5 us -> 50.9 us (0.951)
  Pallas kernels: 21.7 us -> 19.3 us
    pallas_call x6 -> x4, Pallas kernels: 17.5 us -> 15.1 us  [the longest x2 14.9 us: dedisperse(): pl.pallas_call(partial(channel_sums, period=period, hops=hops, build=buil...]
    ppermute x4 -> x3, waiting for transfers between devices: 2.39 us -> 4.13 us  [moved(): lax.ppermute(x, 'chan', [(i, (i + s * cores) % chans) for i in range(chan...]
    ppermute x1, waiting for transfers between devices: 1.33 us -> 0.01 us  [shards(): lax.ppermute(other, 'chan', [(i, i // cores * cores + cores - 1 - i % cor...]
    ppermute x4 -> x3, starting transfers between devices: 6.63 us -> 6.52 us  [moved(): lax.ppermute(x, 'chan', [(i, (i + s * cores) % chans) for i in range(chan...]
  transfers between devices with their start and end apart: 7 -> 6, of which waited for: 3 -> 4; matrix products, arithmetic and copies ran while one was open for 0% -> 0% of each run, Pallas kernels for 21% -> 15%
where the time goes in v4:
time: 50.9 us; the launch traced here: 50.5 us
  Pallas kernels  19.3 us (38%)
  blocking collectives  17.3 us (34%)
  starting transfers between devices  8.72 us (17%)
  waiting for transfers between devices  5.02 us (10%)
    all_to_all x1, blocking collectives, shards(): received = lax.all_to_all(fold(kept, received), 'dm', 0, 0, tiled=True)  17.3 us
    pallas_call x2, Pallas kernels, dedisperse(): pl.pallas_call(partial(channel_sums, period=period, hops=hops, build=buil...  14.9 us
    ppermute x3, starting transfers between devices, moved(): lax.ppermute(x, 'chan', [(i, (i + s * cores) % chans) for i in range(chan...  6.52 us
    pallas_call x2, Pallas kernels, response(): pl.pallas_call(partial(response_kernel, tiles=tiles, edges=len(edges) > 0...  4.17 us
    ppermute x3, waiting for transfers between devices, moved(): lax.ppermute(x, 'chan', [(i, (i + s * cores) % chans) for i in range(chan...  4.13 us
    ppermute x1, starting transfers between devices, shards(): lax.ppermute(head, 'bin', [((i + 1) % bins, i) for i in range(bins)])  1.55 us
  transfers between devices with their start and end apart: 6, of which 4 were waited for; matrix products, arithmetic and copies ran while one was open for 0% of the time, Pallas kernels for 15%

profile of v4, /device:TPU:6, one launch (start us, length us, event | category | flops | bytes accessed | tf_op | source)
XLA Modules:
  0.0 50.5 jit_solution(17994206233516095933)
XLA Ops:
  0.0 0.1 pad_add_fusion.place_ref
  0.1 9.4 %channel_sums.2 = (bf16[4,512,128]{2,1,0:T(8,128)(2,1)S(1)}, bf16[32,2,256,128]{3,2,1,0:T(8,128)(2,1)S(1)}, s32[64,128]{1,0:T(8,128)S(1)}) custom-call(s32[4]{0:T(128)S(1)} %pad_add_fusion.place_ref, s32[64,128]{1,0:T(8,128)} %bitcast.5, bf16[2,4,128,1024]{3,2,1,0:T(8,128)(2,1)} %x_ref.1), custom_call_target="tpu_custom_call" | custom-call | tf_op jit(solution)/shard_map/channel_sums/pallas_call | solution.py:198
  9.4 0.0 copy-start
  9.5 0.1 collective-permute-start
  9.6 5.5 %channel_sums.3.mine_ref = f32[4,512,128]{2,1,0:T(8,128)S(1)} custom-call(s32[4]{0:T(128)S(1)} %pad_add_fusion.place_ref, s32[64,128]{1,0:T(8,128)S(1)} %get-tuple-element.15.delay_ref, bf16[32,2,256,128]{3,2,1,0:T(8,128)(2,1)S(1)} %get-tuple-element.16.x_ref), custom_call_target="tpu_custom_call" | custom-call | tf_op jit(solution)/shard_map/channel_sums/pallas_call | solution.py:198
  15.1 0.0 collective-permute-done.other_ref
  15.1 0.1 join.1
  15.2 3.3 %collective-permute-start.1 = (bf16[512,128]{1,0:T(8,128)(2,1)S(1)}, bf16[512,128]{1,0:T(8,128)(2,1)S(1)}, u32[]{:S(2)}, u32[]{:S(2)}) collective-permute-start(bf16[512,128]{1,0:T(8,128)(2,1)S(1)} %get-tuple-element.19), channel_id=1, source_target_pairs={{0,128},{32,160},{64,192},{96,224},{128,0},{160,32},{192,64},{224,... | collective-permute-start | bytes 393224 | tf_op jit(solution)/shard_map/ppermute | solution.py:385
  18.5 0.7 %collective-permute-start.2 = (bf16[512,128]{1,0:T(8,128)(2,1)S(1)}, bf16[512,128]{1,0:T(8,128)(2,1)S(1)}, u32[]{:S(2)}, u32[]{:S(2)}) collective-permute-start(bf16[512,128]{1,0:T(8,128)(2,1)S(1)} %get-tuple-element.20), channel_id=1, source_target_pairs={{0,64},{32,96},{64,128},{96,160},{128,192},{160,224},{192,0},{224,... | collective-permute-start | bytes 393224 | tf_op jit(solution)/shard_map/ppermute | solution.py:385
  19.1 2.6 %collective-permute-start.3 = (bf16[512,128]{1,0:T(8,128)(2,1)S(1)}, bf16[512,128]{1,0:T(8,128)(2,1)S(1)}, u32[]{:S(2)}, u32[]{:S(2)}) collective-permute-start(bf16[512,128]{1,0:T(8,128)(2,1)S(1)} %get-tuple-element.21), channel_id=1, source_target_pairs={{0,192},{32,224},{64,0},{96,32},{128,64},{160,96},{192,128},{224,1... | collective-permute-start | bytes 393224 | tf_op jit(solution)/shard_map/ppermute | solution.py:385
  21.7 1.4 %collective-permute-done.1.rest_0_ = bf16[512,128]{1,0:T(8,128)(2,1)S(1)} collective-permute-done((bf16[512,128]{1,0:T(8,128)(2,1)S(1)}, bf16[512,128]{1,0:T(8,128)(2,1)S(1)}, u32[]{:S(2)}, u32[]{:S(2)}) %collective-permute-start.1) | collective-permute-done | bytes 131104 | tf_op jit(solution)/shard_map/ppermute | solution.py:385
  23.1 2.5 %collective-permute-done.2.rest_1_ = bf16[512,128]{1,0:T(8,128)(2,1)S(1)} collective-permute-done((bf16[512,128]{1,0:T(8,128)(2,1)S(1)}, bf16[512,128]{1,0:T(8,128)(2,1)S(1)}, u32[]{:S(2)}, u32[]{:S(2)}) %collective-permute-start.2) | collective-permute-done | bytes 131104 | tf_op jit(solution)/shard_map/ppermute | solution.py:385
  25.6 0.2 collective-permute-done.3.rest_2_
  25.8 0.1 fold.1
  25.9 17.3 %all_to_all.5.x_ref = bf16[8,64,128]{2,1,0:T(8,128)(2,1)S(1)} all-to-all(bf16[8,64,128]{2,1,0:T(8,128)(2,1)S(1)} %fold.1), channel_id=1, replica_groups=mesh['chan'=8,'dm'=8,'bin'=4] {'dm'}, dimensions={0} | all-to-all | bytes 262144 | tf_op jit(solution)/shard_map/all_to_all | solution.py:395
  43.3 0.6 %collective-permute-start.4 = (bf16[2,128]{1,0:T(2,128)(2,1)S(1)}, bf16[2,128]{1,0:T(2,128)(2,1)S(1)}, u32[]{:S(2)}, u32[]{:S(2)}) collective-permute-start(bf16[2,128]{1,0:T(2,128)(2,1)S(1)} %get-tuple-element.23), channel_id=1, source_target_pairs={{0,1},{1,2},{2,3},{3,0},{4,5},{5,6},{6,7},{7,4},{8,9},{9,10},{10,1... | collective-permute-start | bytes 1544 | tf_op jit(solution)/shard_map/ppermute | solution.py:398
  43.9 1.6 %collective-permute-start.5 = (bf16[2,128]{1,0:T(2,128)(2,1)S(1)}, bf16[2,128]{1,0:T(2,128)(2,1)S(1)}, u32[]{:S(2)}, u32[]{:S(2)}) collective-permute-start(bf16[2,128]{1,0:T(2,128)(2,1)S(1)} %get-tuple-element.24), channel_id=1, source_target_pairs={{1,0},{2,1},{3,2},{0,3},{5,4},{6,5},{7,6},{4,7},{9,8},{10,9},{11,1... | collective-permute-start | bytes 1544 | tf_op jit(solution)/shard_map/ppermute | solution.py:399
  45.4 0.0 copy-done
  45.4 2.3 %response.2.rest_3_ = bf16[1,64,4,1024]{3,2,1,0:T(4,128)(2,1)} custom-call(s32[4]{0:T(128)S(1)} %pad_add_fusion.place_ref, bf16[64,128]{1,0:T(8,128)(2,1)S(1)} %get-tuple-element.22.y_ref, bf16[2,64,64]{2,1,0:T(8,128)(2,1)S(1)} %copy-done), custom_call_target="tpu_custom_call" | custom-call | tf_op jit(solution)/shard_map/response/pallas_call | solution.py:344
  47.7 0.0 collective-permute-done.4.rest_0_
  47.7 0.9 %collective-permute-done.5.rest_1_ = bf16[2,128]{1,0:T(2,128)(2,1)S(1)} collective-permute-done((bf16[2,128]{1,0:T(2,128)(2,1)S(1)}, bf16[2,128]{1,0:T(2,128)(2,1)S(1)}, u32[]{:S(2)}, u32[]{:S(2)}) %collective-permute-start.5) | collective-permute-done | bytes 544 | tf_op jit(solution)/shard_map/ppermute | solution.py:399
  48.6 1.9 %response.3 = bf16[1,64,4,1024]{3,2,1,0:T(4,128)(2,1)} custom-call(s32[4]{0:T(128)S(1)} %pad_add_fusion.place_ref, bf16[64,128]{1,0:T(8,128)(2,1)S(1)} %get-tuple-element.22.y_ref, bf16[2,128]{1,0:T(2,128)(2,1)S(1)} %collective-permute-done.4.rest_0_, bf16[2,128]{1,0:T(2,128)(2,1)S(1)} %collective-permute-done.5.rest_1_, ...), custom_call_target="tpu_custom_call", output_to_operand_aliasing={{}: (5, {})} | custom-call | tf_op jit(solution)/shard_map/response/pallas_call | solution.py:344
  (1 shorter events, 0.0 us)
Async XLA Ops:
  9.4 36.0 %copy-start = (bf16[2,64,64]{2,1,0:T(8,128)(2,1)S(1)}, bf16[2,64,64]{2,1,0:T(8,128)(2,1)}, u32[]{:S(2)}) copy-start(bf16[2,64,64]{2,1,0:T(8,128)(2,1)} %rest_2_.1) | copy-start | bytes 49156
  9.5 5.6 %collective-permute-start = (bf16[4,512,128]{2,1,0:T(8,128)(2,1)S(1)}, bf16[4,512,128]{2,1,0:T(8,128)(2,1)S(1)}, u32[]{:S(2)}, u32[]{:S(2)}) collective-permute-start(bf16[4,512,128]{2,1,0:T(8,128)(2,1)S(1)} %get-tuple-element.17), channel_id=1, source_target_pairs={{0,32},{32,0},{64,96},{96,64},{128,160},{160,128},{192,224},{224,1... | collective-permute-start | bytes 1572872 | tf_op jit(solution)/shard_map/ppermute | solution.py:388
  15.2 8.0 %collective-permute-start.1 = (bf16[512,128]{1,0:T(8,128)(2,1)S(1)}, bf16[512,128]{1,0:T(8,128)(2,1)S(1)}, u32[]{:S(2)}, u32[]{:S(2)}) collective-permute-start(bf16[512,128]{1,0:T(8,128)(2,1)S(1)} %get-tuple-element.19), channel_id=1, source_target_pairs={{0,128},{32,160},{64,192},{96,224},{128,0},{160,32},{192,64},{224,... | collective-permute-start | bytes 393224 | tf_op jit(solution)/shard_map/ppermute | solution.py:385
  18.5 7.2 %collective-permute-start.2 = (bf16[512,128]{1,0:T(8,128)(2,1)S(1)}, bf16[512,128]{1,0:T(8,128)(2,1)S(1)}, u32[]{:S(2)}, u32[]{:S(2)}) collective-permute-start(bf16[512,128]{1,0:T(8,128)(2,1)S(1)} %get-tuple-element.20), channel_id=1, source_target_pairs={{0,64},{32,96},{64,128},{96,160},{128,192},{160,224},{192,0},{224,... | collective-permute-start | bytes 393224 | tf_op jit(solution)/shard_map/ppermute | solution.py:385
  19.1 6.7 %collective-permute-start.3 = (bf16[512,128]{1,0:T(8,128)(2,1)S(1)}, bf16[512,128]{1,0:T(8,128)(2,1)S(1)}, u32[]{:S(2)}, u32[]{:S(2)}) collective-permute-start(bf16[512,128]{1,0:T(8,128)(2,1)S(1)} %get-tuple-element.21), channel_id=1, source_target_pairs={{0,192},{32,224},{64,0},{96,32},{128,64},{160,96},{192,128},{224,1... | collective-permute-start | bytes 393224 | tf_op jit(solution)/shard_map/ppermute | solution.py:385
  43.3 4.4 %collective-permute-start.4 = (bf16[2,128]{1,0:T(2,128)(2,1)S(1)}, bf16[2,128]{1,0:T(2,128)(2,1)S(1)}, u32[]{:S(2)}, u32[]{:S(2)}) collective-permute-start(bf16[2,128]{1,0:T(2,128)(2,1)S(1)} %get-tuple-element.23), channel_id=1, source_target_pairs={{0,1},{1,2},{2,3},{3,0},{4,5},{5,6},{6,7},{7,4},{8,9},{9,10},{10,1... | collective-permute-start | bytes 1544 | tf_op jit(solution)/shard_map/ppermute | solution.py:398
  43.9 4.8 %collective-permute-start.5 = (bf16[2,128]{1,0:T(2,128)(2,1)S(1)}, bf16[2,128]{1,0:T(2,128)(2,1)S(1)}, u32[]{:S(2)}, u32[]{:S(2)}) collective-permute-start(bf16[2,128]{1,0:T(2,128)(2,1)S(1)} %get-tuple-element.24), channel_id=1, source_target_pairs={{1,0},{2,1},{3,2},{0,3},{5,4},{6,5},{7,6},{4,7},{9,8},{10,9},{11,1... | collective-permute-start | bytes 1544 | tf_op jit(solution)/shard_map/ppermute | solution.py:399

commit v5 on v4

--- a/solution.py
+++ b/solution.py
@@ -17,8 +17,8 @@
 SUB = TILE // GROUP
 LANES = 2 * BEAMS
 PER_HOP = 16
-STEPS = 2
-PIECES = 4
+STEPS = 1
+PIECES = 1
 PHASE_DT = jnp.bfloat16
 F32 = jnp.float32
 BF16 = jnp.bfloat16

time: 50.9 us -> 49.7 us (0.976)
  Pallas kernels: 19.3 us -> 17.9 us
    pallas_call x2, Pallas kernels: 14.9 us -> 13.5 us  [dedisperse(): pl.pallas_call(partial(channel_sums, period=period, hops=hops, build=buil...]
where the time goes in v5:
time: 49.7 us; the launch traced here: 49.3 us
  Pallas kernels  17.9 us (36%)
  blocking collectives  17.3 us (35%)
  starting transfers between devices  8.71 us (18%)
  waiting for transfers between devices  5.02 us (10%)
    all_to_all x1, blocking collectives, shards(): received = lax.all_to_all(fold(kept, received), 'dm', 0, 0, tiled=True)  17.3 us
    pallas_call x2, Pallas kernels, dedisperse(): pl.pallas_call(partial(channel_sums, period=period, hops=hops, build=buil...  13.5 us
    ppermute x3, starting transfers between devices, moved(): lax.ppermute(x, 'chan', [(i, (i + s * cores) % chans) for i in range(chan...  6.52 us
    pallas_call x2, Pallas kernels, response(): pl.pallas_call(partial(response_kernel, tiles=tiles, edges=len(edges) > 0...  4.17 us
    ppermute x3, waiting for transfers between devices, moved(): lax.ppermute(x, 'chan', [(i, (i + s * cores) % chans) for i in range(chan...  4.12 us
    ppermute x1, starting transfers between devices, shards(): lax.ppermute(head, 'bin', [((i + 1) % bins, i) for i in range(bins)])  1.55 us
  transfers between devices with their start and end apart: 6, of which 4 were waited for; matrix products, arithmetic and copies ran while one was open for 0% of the time, Pallas kernels for 15%

profile of v5, /device:TPU:6, one launch (start us, length us, event | category | flops | bytes accessed | tf_op | source)
XLA Modules:
  0.0 49.3 jit_solution(13388831057426453538)
XLA Ops:
  0.0 0.1 pad_add_fusion.place_ref
  0.1 8.3 %channel_sums.2 = (bf16[4,512,128]{2,1,0:T(8,128)(2,1)S(1)}, bf16[32,2,256,128]{3,2,1,0:T(8,128)(2,1)S(1)}, s32[64,128]{1,0:T(8,128)S(1)}) custom-call(s32[4]{0:T(128)S(1)} %pad_add_fusion.place_ref, s32[64,128]{1,0:T(8,128)} %bitcast.5, bf16[2,4,128,1024]{3,2,1,0:T(8,128)(2,1)} %x_ref.1), custom_call_target="tpu_custom_call" | custom-call | tf_op jit(solution)/shard_map/channel_sums/pallas_call | solution.py:198
  8.4 0.0 copy-start
  8.4 0.1 collective-permute-start
  8.5 5.2 %channel_sums.3.mine_ref = f32[4,512,128]{2,1,0:T(8,128)S(1)} custom-call(s32[4]{0:T(128)S(1)} %pad_add_fusion.place_ref, s32[64,128]{1,0:T(8,128)S(1)} %get-tuple-element.15.delay_ref, bf16[32,2,256,128]{3,2,1,0:T(8,128)(2,1)S(1)} %get-tuple-element.16.x_ref), custom_call_target="tpu_custom_call" | custom-call | tf_op jit(solution)/shard_map/channel_sums/pallas_call | solution.py:198
  13.7 0.0 collective-permute-done.other_ref
  13.7 0.1 join.1
  13.8 3.3 %collective-permute-start.1 = (bf16[512,128]{1,0:T(8,128)(2,1)S(1)}, bf16[512,128]{1,0:T(8,128)(2,1)S(1)}, u32[]{:S(2)}, u32[]{:S(2)}) collective-permute-start(bf16[512,128]{1,0:T(8,128)(2,1)S(1)} %get-tuple-element.19), channel_id=1, source_target_pairs={{0,128},{32,160},{64,192},{96,224},{128,0},{160,32},{192,64},{224,... | collective-permute-start | bytes 393224 | tf_op jit(solution)/shard_map/ppermute | solution.py:385
  17.1 0.7 %collective-permute-start.2 = (bf16[512,128]{1,0:T(8,128)(2,1)S(1)}, bf16[512,128]{1,0:T(8,128)(2,1)S(1)}, u32[]{:S(2)}, u32[]{:S(2)}) collective-permute-start(bf16[512,128]{1,0:T(8,128)(2,1)S(1)} %get-tuple-element.20), channel_id=1, source_target_pairs={{0,64},{32,96},{64,128},{96,160},{128,192},{160,224},{192,0},{224,... | collective-permute-start | bytes 393224 | tf_op jit(solution)/shard_map/ppermute | solution.py:385
  17.8 2.6 %collective-permute-start.3 = (bf16[512,128]{1,0:T(8,128)(2,1)S(1)}, bf16[512,128]{1,0:T(8,128)(2,1)S(1)}, u32[]{:S(2)}, u32[]{:S(2)}) collective-permute-start(bf16[512,128]{1,0:T(8,128)(2,1)S(1)} %get-tuple-element.21), channel_id=1, source_target_pairs={{0,192},{32,224},{64,0},{96,32},{128,64},{160,96},{192,128},{224,1... | collective-permute-start | bytes 393224 | tf_op jit(solution)/shard_map/ppermute | solution.py:385
  20.3 1.4 %collective-permute-done.1.rest_0_ = bf16[512,128]{1,0:T(8,128)(2,1)S(1)} collective-permute-done((bf16[512,128]{1,0:T(8,128)(2,1)S(1)}, bf16[512,128]{1,0:T(8,128)(2,1)S(1)}, u32[]{:S(2)}, u32[]{:S(2)}) %collective-permute-start.1) | collective-permute-done | bytes 131104 | tf_op jit(solution)/shard_map/ppermute | solution.py:385
  21.8 2.5 %collective-permute-done.2.rest_1_ = bf16[512,128]{1,0:T(8,128)(2,1)S(1)} collective-permute-done((bf16[512,128]{1,0:T(8,128)(2,1)S(1)}, bf16[512,128]{1,0:T(8,128)(2,1)S(1)}, u32[]{:S(2)}, u32[]{:S(2)}) %collective-permute-start.2) | collective-permute-done | bytes 131104 | tf_op jit(solution)/shard_map/ppermute | solution.py:385
  24.3 0.2 collective-permute-done.3.rest_2_
  24.5 0.1 fold.1
  24.6 17.3 %all_to_all.5.x_ref = bf16[8,64,128]{2,1,0:T(8,128)(2,1)S(1)} all-to-all(bf16[8,64,128]{2,1,0:T(8,128)(2,1)S(1)} %fold.1), channel_id=1, replica_groups=mesh['chan'=8,'dm'=8,'bin'=4] {'dm'}, dimensions={0} | all-to-all | bytes 262144 | tf_op jit(solution)/shard_map/all_to_all | solution.py:395
  41.9 0.6 %collective-permute-start.4 = (bf16[2,128]{1,0:T(2,128)(2,1)S(1)}, bf16[2,128]{1,0:T(2,128)(2,1)S(1)}, u32[]{:S(2)}, u32[]{:S(2)}) collective-permute-start(bf16[2,128]{1,0:T(2,128)(2,1)S(1)} %get-tuple-element.23), channel_id=1, source_target_pairs={{0,1},{1,2},{2,3},{3,0},{4,5},{5,6},{6,7},{7,4},{8,9},{9,10},{10,1... | collective-permute-start | bytes 1544 | tf_op jit(solution)/shard_map/ppermute | solution.py:398
  42.5 1.5 %collective-permute-start.5 = (bf16[2,128]{1,0:T(2,128)(2,1)S(1)}, bf16[2,128]{1,0:T(2,128)(2,1)S(1)}, u32[]{:S(2)}, u32[]{:S(2)}) collective-permute-start(bf16[2,128]{1,0:T(2,128)(2,1)S(1)} %get-tuple-element.24), channel_id=1, source_target_pairs={{1,0},{2,1},{3,2},{0,3},{5,4},{6,5},{7,6},{4,7},{9,8},{10,9},{11,1... | collective-permute-start | bytes 1544 | tf_op jit(solution)/shard_map/ppermute | solution.py:399
  44.1 0.0 copy-done
  44.1 2.3 %response.2.rest_3_ = bf16[1,64,4,1024]{3,2,1,0:T(4,128)(2,1)} custom-call(s32[4]{0:T(128)S(1)} %pad_add_fusion.place_ref, bf16[64,128]{1,0:T(8,128)(2,1)S(1)} %get-tuple-element.22.y_ref, bf16[2,64,64]{2,1,0:T(8,128)(2,1)S(1)} %copy-done), custom_call_target="tpu_custom_call" | custom-call | tf_op jit(solution)/shard_map/response/pallas_call | solution.py:344
  46.4 0.0 collective-permute-done.4.rest_0_
  46.4 0.9 %collective-permute-done.5.rest_1_ = bf16[2,128]{1,0:T(2,128)(2,1)S(1)} collective-permute-done((bf16[2,128]{1,0:T(2,128)(2,1)S(1)}, bf16[2,128]{1,0:T(2,128)(2,1)S(1)}, u32[]{:S(2)}, u32[]{:S(2)}) %collective-permute-start.5) | collective-permute-done | bytes 544 | tf_op jit(solution)/shard_map/ppermute | solution.py:399
  47.3 1.9 %response.3 = bf16[1,64,4,1024]{3,2,1,0:T(4,128)(2,1)} custom-call(s32[4]{0:T(128)S(1)} %pad_add_fusion.place_ref, bf16[64,128]{1,0:T(8,128)(2,1)S(1)} %get-tuple-element.22.y_ref, bf16[2,128]{1,0:T(2,128)(2,1)S(1)} %collective-permute-done.4.rest_0_, bf16[2,128]{1,0:T(2,128)(2,1)S(1)} %collective-permute-done.5.rest_1_, ...), custom_call_target="tpu_custom_call", output_to_operand_aliasing={{}: (5, {})} | custom-call | tf_op jit(solution)/shard_map/response/pallas_call | solution.py:344
  (1 shorter events, 0.0 us)
Async XLA Ops:
  8.4 35.7 %copy-start = (bf16[2,64,64]{2,1,0:T(8,128)(2,1)S(1)}, bf16[2,64,64]{2,1,0:T(8,128)(2,1)}, u32[]{:S(2)}) copy-start(bf16[2,64,64]{2,1,0:T(8,128)(2,1)} %rest_2_.1) | copy-start | bytes 49156
  8.4 5.3 %collective-permute-start = (bf16[4,512,128]{2,1,0:T(8,128)(2,1)S(1)}, bf16[4,512,128]{2,1,0:T(8,128)(2,1)S(1)}, u32[]{:S(2)}, u32[]{:S(2)}) collective-permute-start(bf16[4,512,128]{2,1,0:T(8,128)(2,1)S(1)} %get-tuple-element.17), channel_id=1, source_target_pairs={{0,32},{32,0},{64,96},{96,64},{128,160},{160,128},{192,224},{224,1... | collective-permute-start | bytes 1572872 | tf_op jit(solution)/shard_map/ppermute | solution.py:388
  13.8 8.0 %collective-permute-start.1 = (bf16[512,128]{1,0:T(8,128)(2,1)S(1)}, bf16[512,128]{1,0:T(8,128)(2,1)S(1)}, u32[]{:S(2)}, u32[]{:S(2)}) collective-permute-start(bf16[512,128]{1,0:T(8,128)(2,1)S(1)} %get-tuple-element.19), channel_id=1, source_target_pairs={{0,128},{32,160},{64,192},{96,224},{128,0},{160,32},{192,64},{224,... | collective-permute-start | bytes 393224 | tf_op jit(solution)/shard_map/ppermute | solution.py:385
  17.1 7.2 %collective-permute-start.2 = (bf16[512,128]{1,0:T(8,128)(2,1)S(1)}, bf16[512,128]{1,0:T(8,128)(2,1)S(1)}, u32[]{:S(2)}, u32[]{:S(2)}) collective-permute-start(bf16[512,128]{1,0:T(8,128)(2,1)S(1)} %get-tuple-element.20), channel_id=1, source_target_pairs={{0,64},{32,96},{64,128},{96,160},{128,192},{160,224},{192,0},{224,... | collective-permute-start | bytes 393224 | tf_op jit(solution)/shard_map/ppermute | solution.py:385
  17.8 6.7 %collective-permute-start.3 = (bf16[512,128]{1,0:T(8,128)(2,1)S(1)}, bf16[512,128]{1,0:T(8,128)(2,1)S(1)}, u32[]{:S(2)}, u32[]{:S(2)}) collective-permute-start(bf16[512,128]{1,0:T(8,128)(2,1)S(1)} %get-tuple-element.21), channel_id=1, source_target_pairs={{0,192},{32,224},{64,0},{96,32},{128,64},{160,96},{192,128},{224,1... | collective-permute-start | bytes 393224 | tf_op jit(solution)/shard_map/ppermute | solution.py:385
  41.9 4.4 %collective-permute-start.4 = (bf16[2,128]{1,0:T(2,128)(2,1)S(1)}, bf16[2,128]{1,0:T(2,128)(2,1)S(1)}, u32[]{:S(2)}, u32[]{:S(2)}) collective-permute-start(bf16[2,128]{1,0:T(2,128)(2,1)S(1)} %get-tuple-element.23), channel_id=1, source_target_pairs={{0,1},{1,2},{2,3},{3,0},{4,5},{5,6},{6,7},{7,4},{8,9},{9,10},{10,1... | collective-permute-start | bytes 1544 | tf_op jit(solution)/shard_map/ppermute | solution.py:398
  42.5 4.8 %collective-permute-start.5 = (bf16[2,128]{1,0:T(2,128)(2,1)S(1)}, bf16[2,128]{1,0:T(2,128)(2,1)S(1)}, u32[]{:S(2)}, u32[]{:S(2)}) collective-permute-start(bf16[2,128]{1,0:T(2,128)(2,1)S(1)} %get-tuple-element.24), channel_id=1, source_target_pairs={{1,0},{2,1},{3,2},{0,3},{5,4},{6,5},{7,6},{4,7},{9,8},{10,9},{11,1... | collective-permute-start | bytes 1544 | tf_op jit(solution)/shard_map/ppermute | solution.py:399

commit v6 on v5

--- a/solution.py
+++ b/solution.py
@@ -286,9 +286,9 @@
 
 def response_kernel(place_ref, y_ref, *rest, tiles, edges):
     if edges:
-        left_ref, right_ref, h_ref, _, out_ref, u_ref, win_ref, pow_ref, part_ref, sems = rest
+        left_ref, right_ref, h_ref, _, out_ref, final_ref, u_ref, win_ref, pow_ref, sem = rest
     else:
-        h_ref, out_ref, u_ref, win_ref, pow_ref, part_ref, sems = rest
+        h_ref, out_ref, u_ref, win_ref, pow_ref = rest
     rows = y_ref.shape[0]
     edge = TAPS // 2 // GROUP
     u_ref[...] = jnp.zeros(u_ref.shape, F32)
@@ -321,17 +321,12 @@
         power = re * re + im * im
         for i in range(len(tiles)):
             pow_ref[pl.ds(i * size + beam, TEMPLATES, stride=BEAMS), :] = power[:, i * TILE : (i + 1) * TILE]
-    copies = []
     for i, m in enumerate(tiles):
         part = pow_ref[pl.ds(i * size, size), :]
-        part_ref[i] = part.reshape(TEMPLATES, BEAMS, TILE).astype(BF16)
-        copies.append(
-            pltpu.make_async_copy(
-                part_ref.at[i], out_ref.at[0, :, :, pl.ds(m * TILE, TILE)], sems.at[i]
-            )
-        )
-        copies[-1].start()
-    for copy in copies:
+        out_ref[0, :, :, pl.ds(m * TILE, TILE)] = part.reshape(TEMPLATES, BEAMS, TILE).astype(BF16)
+    if edges:
+        copy = pltpu.make_async_copy(out_ref, final_ref, sem)
+        copy.start()
         copy.wait()
 
 
@@ -340,26 +335,26 @@
     count = len(tiles)
     vmem = pl.BlockSpec(memory_space=pltpu.VMEM)
     hbm = pl.BlockSpec(memory_space=pl.ANY)
+    shape = (1, TEMPLATES, BEAMS, width)
     inputs = [near(y), *map(near, edges), templates]
     return pl.pallas_call(
         partial(response_kernel, tiles=tiles, edges=len(edges) > 0),
         grid_spec=pltpu.PrefetchScalarGridSpec(
             num_scalar_prefetch=1,
-            in_specs=[vmem] * len(inputs) + [hbm] * len(before),
-            out_specs=hbm,
+            in_specs=[vmem] * (len(inputs) + len(before)),
+            out_specs=[vmem] + [hbm] * len(before),
             scratch_shapes=[
                 pltpu.VMEM((16 * SUB, TILE), F32),
                 pltpu.VMEM((BEAMS, 2 * TAPS, count * TILE), BF16),
                 pltpu.VMEM((TEMPLATES * BEAMS * count, TILE), F32),
-                pltpu.VMEM((count, TEMPLATES, BEAMS, TILE), BF16),
-                pltpu.SemaphoreType.DMA((count,)),
-            ],
+            ]
+            + [pltpu.SemaphoreType.DMA] * len(before),
         ),
-        out_shape=jax.ShapeDtypeStruct((1, TEMPLATES, BEAMS, width), BF16),
+        out_shape=[pltpu.VMEM(shape, BF16)] + [jax.ShapeDtypeStruct(shape, BF16)] * len(before),
         input_output_aliases={1 + len(inputs): 0} if before else {},
         compiler_params=pltpu.CompilerParams(vmem_limit_bytes=24 * 2**20),
         name="response",
-    )(place, *inputs, *before)
+    )(place, *inputs, *map(near, before))[-1]
 
 
 def shards(spectra, delays, templates):

time: 49.7 us -> 49.7 us (level)
  waiting for transfers between devices: 5.02 us -> 5.76 us
  Pallas kernels: 17.9 us -> 17.3 us
    ppermute x1, waiting for transfers between devices: 0.9 us -> 1.64 us  [shards(): lax.ppermute(head, 'bin', [((i + 1) % bins, i) for i in range(bins)])]
    pallas_call x2, Pallas kernels: 4.17 us -> 3.58 us  [response(): pl.pallas_call(partial(response_kernel, tiles=tiles, edges=len(edges) > 0...]
  transfers between devices with their start and end apart: 6 -> 6, of which waited for: 4 -> 4; matrix products, arithmetic and copies ran while one was open for 0% -> 0% of each run, Pallas kernels for 15% -> 14%
where the time goes in v6:
time: 49.7 us; the launch traced here: 49.4 us
  Pallas kernels  17.3 us (35%)
  blocking collectives  17.3 us (35%)
  starting transfers between devices  8.71 us (18%)
  waiting for transfers between devices  5.76 us (12%)
    all_to_all x1, blocking collectives, shards(): received = lax.all_to_all(fold(kept, received), 'dm', 0, 0, tiled=True)  17.3 us
    pallas_call x2, Pallas kernels, dedisperse(): pl.pallas_call(partial(channel_sums, period=period, hops=hops, build=buil...  13.5 us
    ppermute x3, starting transfers between devices, moved(): lax.ppermute(x, 'chan', [(i, (i + s * cores) % chans) for i in range(chan...  6.52 us
    ppermute x3, waiting for transfers between devices, moved(): lax.ppermute(x, 'chan', [(i, (i + s * cores) % chans) for i in range(chan...  4.12 us
    pallas_call x2, Pallas kernels, response(): pl.pallas_call(partial(response_kernel, tiles=tiles, edges=len(edges) > 0...  3.58 us
    ppermute x1, waiting for transfers between devices, shards(): lax.ppermute(head, 'bin', [((i + 1) % bins, i) for i in range(bins)])  1.64 us
    ppermute x1, starting transfers between devices, shards(): lax.ppermute(head, 'bin', [((i + 1) % bins, i) for i in range(bins)])  1.55 us
  transfers between devices with their start and end apart: 6, of which 4 were waited for; matrix products, arithmetic and copies ran while one was open for 0% of the time, Pallas kernels for 14%

profile of v6, /device:TPU:6, one launch (start us, length us, event | category | flops | bytes accessed | tf_op | source)
XLA Modules:
  0.0 49.4 jit_solution(11539063379657439104)
XLA Ops:
  0.0 0.1 pad_add_fusion.place_ref
  0.1 8.3 %channel_sums.2 = (bf16[4,512,128]{2,1,0:T(8,128)(2,1)S(1)}, bf16[32,2,256,128]{3,2,1,0:T(8,128)(2,1)S(1)}, s32[64,128]{1,0:T(8,128)S(1)}) custom-call(s32[4]{0:T(128)S(1)} %pad_add_fusion.place_ref, s32[64,128]{1,0:T(8,128)} %bitcast.5, bf16[2,4,128,1024]{3,2,1,0:T(8,128)(2,1)} %x_ref.1), custom_call_target="tpu_custom_call" | custom-call | tf_op jit(solution)/shard_map/channel_sums/pallas_call | solution.py:198
  8.4 0.0 copy-start
  8.4 0.1 collective-permute-start
  8.5 5.2 %channel_sums.3.mine_ref = f32[4,512,128]{2,1,0:T(8,128)S(1)} custom-call(s32[4]{0:T(128)S(1)} %pad_add_fusion.place_ref, s32[64,128]{1,0:T(8,128)S(1)} %get-tuple-element.16.delay_ref, bf16[32,2,256,128]{3,2,1,0:T(8,128)(2,1)S(1)} %get-tuple-element.17.x_ref), custom_call_target="tpu_custom_call" | custom-call | tf_op jit(solution)/shard_map/channel_sums/pallas_call | solution.py:198
  13.7 0.0 collective-permute-done.other_ref
  13.7 0.1 join.1
  13.8 3.3 %collective-permute-start.1 = (bf16[512,128]{1,0:T(8,128)(2,1)S(1)}, bf16[512,128]{1,0:T(8,128)(2,1)S(1)}, u32[]{:S(2)}, u32[]{:S(2)}) collective-permute-start(bf16[512,128]{1,0:T(8,128)(2,1)S(1)} %get-tuple-element.20), channel_id=1, source_target_pairs={{0,128},{32,160},{64,192},{96,224},{128,0},{160,32},{192,64},{224,... | collective-permute-start | bytes 393224 | tf_op jit(solution)/shard_map/ppermute | solution.py:380
  17.1 0.7 %collective-permute-start.2 = (bf16[512,128]{1,0:T(8,128)(2,1)S(1)}, bf16[512,128]{1,0:T(8,128)(2,1)S(1)}, u32[]{:S(2)}, u32[]{:S(2)}) collective-permute-start(bf16[512,128]{1,0:T(8,128)(2,1)S(1)} %get-tuple-element.21), channel_id=1, source_target_pairs={{0,64},{32,96},{64,128},{96,160},{128,192},{160,224},{192,0},{224,... | collective-permute-start | bytes 393224 | tf_op jit(solution)/shard_map/ppermute | solution.py:380
  17.8 2.6 %collective-permute-start.3 = (bf16[512,128]{1,0:T(8,128)(2,1)S(1)}, bf16[512,128]{1,0:T(8,128)(2,1)S(1)}, u32[]{:S(2)}, u32[]{:S(2)}) collective-permute-start(bf16[512,128]{1,0:T(8,128)(2,1)S(1)} %get-tuple-element.22), channel_id=1, source_target_pairs={{0,192},{32,224},{64,0},{96,32},{128,64},{160,96},{192,128},{224,1... | collective-permute-start | bytes 393224 | tf_op jit(solution)/shard_map/ppermute | solution.py:380
  20.3 1.4 %collective-permute-done.1.rest_0_ = bf16[512,128]{1,0:T(8,128)(2,1)S(1)} collective-permute-done((bf16[512,128]{1,0:T(8,128)(2,1)S(1)}, bf16[512,128]{1,0:T(8,128)(2,1)S(1)}, u32[]{:S(2)}, u32[]{:S(2)}) %collective-permute-start.1) | collective-permute-done | bytes 131104 | tf_op jit(solution)/shard_map/ppermute | solution.py:380
  21.8 2.5 %collective-permute-done.2.rest_1_ = bf16[512,128]{1,0:T(8,128)(2,1)S(1)} collective-permute-done((bf16[512,128]{1,0:T(8,128)(2,1)S(1)}, bf16[512,128]{1,0:T(8,128)(2,1)S(1)}, u32[]{:S(2)}, u32[]{:S(2)}) %collective-permute-start.2) | collective-permute-done | bytes 131104 | tf_op jit(solution)/shard_map/ppermute | solution.py:380
  24.3 0.2 collective-permute-done.3.rest_2_
  24.5 0.1 fold.1
  24.6 17.3 %all_to_all.5.x_ref = bf16[8,64,128]{2,1,0:T(8,128)(2,1)S(1)} all-to-all(bf16[8,64,128]{2,1,0:T(8,128)(2,1)S(1)} %fold.1), channel_id=1, replica_groups=mesh['chan'=8,'dm'=8,'bin'=4] {'dm'}, dimensions={0} | all-to-all | bytes 262144 | tf_op jit(solution)/shard_map/all_to_all | solution.py:390
  41.9 0.6 %collective-permute-start.4 = (bf16[2,128]{1,0:T(2,128)(2,1)S(1)}, bf16[2,128]{1,0:T(2,128)(2,1)S(1)}, u32[]{:S(2)}, u32[]{:S(2)}) collective-permute-start(bf16[2,128]{1,0:T(2,128)(2,1)S(1)} %get-tuple-element.24), channel_id=1, source_target_pairs={{0,1},{1,2},{2,3},{3,0},{4,5},{5,6},{6,7},{7,4},{8,9},{9,10},{10,1... | collective-permute-start | bytes 1544 | tf_op jit(solution)/shard_map/ppermute | solution.py:393
  42.5 1.5 %collective-permute-start.5 = (bf16[2,128]{1,0:T(2,128)(2,1)S(1)}, bf16[2,128]{1,0:T(2,128)(2,1)S(1)}, u32[]{:S(2)}, u32[]{:S(2)}) collective-permute-start(bf16[2,128]{1,0:T(2,128)(2,1)S(1)} %get-tuple-element.25), channel_id=1, source_target_pairs={{1,0},{2,1},{3,2},{0,3},{5,4},{6,5},{7,6},{4,7},{9,8},{10,9},{11,1... | collective-permute-start | bytes 1544 | tf_op jit(solution)/shard_map/ppermute | solution.py:394
  44.1 0.0 copy-done
  44.1 1.6 %response.2.rest_3_ = bf16[1,64,4,1024]{3,2,1,0:T(4,128)(2,1)S(1)} custom-call(s32[4]{0:T(128)S(1)} %pad_add_fusion.place_ref, bf16[64,128]{1,0:T(8,128)(2,1)S(1)} %get-tuple-element.23.y_ref, bf16[2,64,64]{2,1,0:T(8,128)(2,1)S(1)} %copy-done), custom_call_target="tpu_custom_call" | custom-call | tf_op jit(solution)/shard_map/response/pallas_call | solution.py:340
  45.6 0.0 collective-permute-done.4.rest_0_
  45.6 1.6 %collective-permute-done.5.rest_1_ = bf16[2,128]{1,0:T(2,128)(2,1)S(1)} collective-permute-done((bf16[2,128]{1,0:T(2,128)(2,1)S(1)}, bf16[2,128]{1,0:T(2,128)(2,1)S(1)}, u32[]{:S(2)}, u32[]{:S(2)}) %collective-permute-start.5) | collective-permute-done | bytes 544 | tf_op jit(solution)/shard_map/ppermute | solution.py:394
  47.3 2.0 %response.3 = (bf16[1,64,4,1024]{3,2,1,0:T(4,128)(2,1)S(1)}, bf16[1,64,4,1024]{3,2,1,0:T(4,128)(2,1)}) custom-call(s32[4]{0:T(128)S(1)} %pad_add_fusion.place_ref, bf16[64,128]{1,0:T(8,128)(2,1)S(1)} %get-tuple-element.23.y_ref, bf16[2,128]{1,0:T(2,128)(2,1)S(1)} %collective-permute-done.4.rest_0_, ...), custom_call_target="tpu_custom_call", output_to_operand_aliasing={{0}: (5, {})} | custom-call | tf_op jit(solution)/shard_map/response/pallas_call | solution.py:340
  (1 shorter events, 0.0 us)
Async XLA Ops:
  8.4 35.7 %copy-start = (bf16[2,64,64]{2,1,0:T(8,128)(2,1)S(1)}, bf16[2,64,64]{2,1,0:T(8,128)(2,1)}, u32[]{:S(2)}) copy-start(bf16[2,64,64]{2,1,0:T(8,128)(2,1)} %rest_2_.1) | copy-start | bytes 49156
  8.4 5.3 %collective-permute-start = (bf16[4,512,128]{2,1,0:T(8,128)(2,1)S(1)}, bf16[4,512,128]{2,1,0:T(8,128)(2,1)S(1)}, u32[]{:S(2)}, u32[]{:S(2)}) collective-permute-start(bf16[4,512,128]{2,1,0:T(8,128)(2,1)S(1)} %get-tuple-element.18), channel_id=1, source_target_pairs={{0,32},{32,0},{64,96},{96,64},{128,160},{160,128},{192,224},{224,1... | collective-permute-start | bytes 1572872 | tf_op jit(solution)/shard_map/ppermute | solution.py:383
  13.8 8.0 %collective-permute-start.1 = (bf16[512,128]{1,0:T(8,128)(2,1)S(1)}, bf16[512,128]{1,0:T(8,128)(2,1)S(1)}, u32[]{:S(2)}, u32[]{:S(2)}) collective-permute-start(bf16[512,128]{1,0:T(8,128)(2,1)S(1)} %get-tuple-element.20), channel_id=1, source_target_pairs={{0,128},{32,160},{64,192},{96,224},{128,0},{160,32},{192,64},{224,... | collective-permute-start | bytes 393224 | tf_op jit(solution)/shard_map/ppermute | solution.py:380
  17.1 7.2 %collective-permute-start.2 = (bf16[512,128]{1,0:T(8,128)(2,1)S(1)}, bf16[512,128]{1,0:T(8,128)(2,1)S(1)}, u32[]{:S(2)}, u32[]{:S(2)}) collective-permute-start(bf16[512,128]{1,0:T(8,128)(2,1)S(1)} %get-tuple-element.21), channel_id=1, source_target_pairs={{0,64},{32,96},{64,128},{96,160},{128,192},{160,224},{192,0},{224,... | collective-permute-start | bytes 393224 | tf_op jit(solution)/shard_map/ppermute | solution.py:380
  17.8 6.7 %collective-permute-start.3 = (bf16[512,128]{1,0:T(8,128)(2,1)S(1)}, bf16[512,128]{1,0:T(8,128)(2,1)S(1)}, u32[]{:S(2)}, u32[]{:S(2)}) collective-permute-start(bf16[512,128]{1,0:T(8,128)(2,1)S(1)} %get-tuple-element.22), channel_id=1, source_target_pairs={{0,192},{32,224},{64,0},{96,32},{128,64},{160,96},{192,128},{224,1... | collective-permute-start | bytes 393224 | tf_op jit(solution)/shard_map/ppermute | solution.py:380
  41.9 3.7 %collective-permute-start.4 = (bf16[2,128]{1,0:T(2,128)(2,1)S(1)}, bf16[2,128]{1,0:T(2,128)(2,1)S(1)}, u32[]{:S(2)}, u32[]{:S(2)}) collective-permute-start(bf16[2,128]{1,0:T(2,128)(2,1)S(1)} %get-tuple-element.24), channel_id=1, source_target_pairs={{0,1},{1,2},{2,3},{3,0},{4,5},{5,6},{6,7},{7,4},{8,9},{9,10},{10,1... | collective-permute-start | bytes 1544 | tf_op jit(solution)/shard_map/ppermute | solution.py:393
  42.5 4.8 %collective-permute-start.5 = (bf16[2,128]{1,0:T(2,128)(2,1)S(1)}, bf16[2,128]{1,0:T(2,128)(2,1)S(1)}, u32[]{:S(2)}, u32[]{:S(2)}) collective-permute-start(bf16[2,128]{1,0:T(2,128)(2,1)S(1)} %get-tuple-element.25), channel_id=1, source_target_pairs={{1,0},{2,1},{3,2},{0,3},{5,4},{6,5},{7,6},{4,7},{9,8},{10,9},{11,1... | collective-permute-start | bytes 1544 | tf_op jit(solution)/shard_map/ppermute | solution.py:394
